TPU v7x, 256 devices: a whole 4x4x8 slice. The times are simulated.
256 devices in a mesh: ep: 64 (over z, x, core), tp: 4 (over y).
Axes of the slice: x: 4, y: 4, z: 8, core: 2. Of those that a mesh axis runs over, the one named last changes fastest.
Arguments:
- hidden_in: bfloat16 [8192, 2048], P('ep', 'tp'), may hold values from -50 to 50
- norm_gain: float32 [2048], P('tp'), may hold values from 0.5 to 1.5
- expert_ids: int32 [8192, 8], P('ep'), may hold values from 0 to 127, all different within a row; in each aligned block of 128 rows (0 to 127, 128 to 255, ...) at most 12 rows name the same one
- routing_weight: float32 [8192, 8], P('ep'), may hold values from 0.03 to 0.3
- labels: int32 [8192], P('ep'), may hold values from 0 to 3
- grad_later: bfloat16 [8192, 2048], P('ep', 'tp'), may hold values from -6 to 6
- head_weight: bfloat16 [2048, 4], P('tp'), may hold values from -0.125 to 0.125
- gate_weight: bfloat16 [98304, 2048], P(('ep', 'tp')), may hold values from -0.125 to 0.125
- up_weight: bfloat16 [98304, 2048], P(('ep', 'tp')), may hold values from -0.125 to 0.125
- down_weight: bfloat16 [98304, 2048], P(('ep', 'tp')), may hold values from -0.21875 to 0.21875
Outputs:
- token_loss: float32 [8192], P('ep')
- outcome: bfloat16 [8192, 2048], P('ep', 'tp')
- grad_input: bfloat16 [8192, 2048], P('ep', 'tp')
- grad_gate: bfloat16 [98304, 2048], P(('ep', 'tp'))
- grad_up: bfloat16 [98304, 2048], P(('ep', 'tp'))
- grad_down: bfloat16 [98304, 2048], P(('ep', 'tp'))
Inputs may be any that keep to these rules, and one draw needn't show every extreme that they name: `expert_ids`: each row names 8 different experts. Within the 128 rows of one index of ep, no expert is named more than 12 times, a bound that some block reaches.
All inputs are finite; a program needn't handle non-finite values.
Results may differ from a plain program's by a relative error of at most 0.011.
Values may be sent and summed in bfloat16 or wider, within the bound.
A program may use at most 128 MiB of HBM per device.

v0:
```python
import jax
import jax.numpy as jnp
from jax import lax
from jax.sharding import PartitionSpec as P

FF = 768


EPS = 1e-06
LOSS_SCALE = 64.0


def slot_targets(expert_ids, expert_count, capacity):
    flat_ids = expert_ids.reshape(-1)
    marks = (flat_ids[:, None] == jnp.arange(expert_count, dtype=jnp.int32)[None, :]).astype(
        jnp.int32
    )
    before = jnp.cumsum(marks, axis=0) - marks
    slot_pos = jnp.sum(before * marks, axis=1)
    return flat_ids * capacity + slot_pos


def fill_slots(token_rows, scales, targets, slot_count, top_count):
    repeated = jnp.repeat(token_rows, top_count, axis=0)
    if scales is not None:
        repeated = (scales[:, None] * repeated.astype(jnp.float32)).astype(jnp.bfloat16)
    blank = jnp.zeros((slot_count, token_rows.shape[1]), jnp.bfloat16)
    return blank.at[targets].set(repeated)


def dispatch(token_rows, scales, targets, layout, first_local, held):
    dev_count, local_count, capacity, slot_count, top_count = layout
    whole_rows = lax.all_gather(token_rows, "tp", axis=1, tiled=True)
    width = whole_rows.shape[1]
    filled = fill_slots(whole_rows, scales, targets, slot_count, top_count)
    filled = filled.reshape(dev_count, local_count, capacity, width)
    outgoing = lax.dynamic_slice_in_dim(filled, first_local, held, 1).reshape(
        dev_count, held * capacity, width
    )
    arrived = lax.all_to_all(outgoing, "ep", split_axis=0, concat_axis=0, tiled=True)
    return arrived.reshape(dev_count, held, capacity, width)


def combine(partial_value, scales, targets, layout, first_local, held):
    dev_count, local_count, capacity, slot_count, top_count = layout
    tok_count = targets.shape[0] // top_count
    width = partial_value.shape[3]
    outgoing = partial_value.astype(jnp.bfloat16).reshape(dev_count, held * capacity, width)
    returned = lax.all_to_all(outgoing, "ep", split_axis=0, concat_axis=0, tiled=True)
    flat_rows = returned.reshape(-1, width)
    expert = targets // capacity
    slot_pos = targets % capacity
    owner = expert // local_count
    relative = expert % local_count - first_local
    owned = jnp.logical_and(relative >= 0, relative < held)
    rows = owner * (held * capacity) + jnp.clip(relative, 0, held - 1) * capacity + slot_pos
    factor = owned.astype(jnp.float32)
    if scales is not None:
        factor = factor * scales
    picked = flat_rows[rows].astype(jnp.float32) * factor[:, None]
    summed = jnp.sum(picked.reshape(tok_count, top_count, width), axis=1)
    return lax.psum_scatter(summed, "tp", scatter_dimension=1, tiled=True)


def shards(
    hidden_in,
    norm_gain,
    expert_ids,
    routing_weight,
    labels,
    grad_later,
    head_weight,
    gate_weight,
    up_weight,
    down_weight,
):
    dev_count = lax.axis_size("ep")
    group_count = lax.axis_size("tp")
    tok_count = hidden_in.shape[0]
    top_count = expert_ids.shape[1]
    model_width = gate_weight.shape[1]
    unit_rows = gate_weight.shape[0]
    local_count = unit_rows * group_count // FF
    expert_count = local_count * dev_count
    group_units = min(unit_rows, FF)
    held = unit_rows // group_units
    first_local = lax.axis_index("tp") * unit_rows // FF
    capacity = tok_count * top_count * 3 // (2 * expert_count)
    slot_count = expert_count * capacity
    layout = (dev_count, local_count, capacity, slot_count, top_count)
    targets = slot_targets(expert_ids, expert_count, capacity)
    scales = routing_weight.reshape(-1)
    w_gate = gate_weight.reshape(held, group_units, model_width)
    w_up = up_weight.reshape(held, group_units, model_width)
    w_down = down_weight.reshape(held, group_units, model_width)
    hidden_wide = hidden_in.astype(jnp.float32)
    squares = lax.psum(jnp.sum(hidden_wide * hidden_wide, axis=1), "tp")
    inv_rms = lax.rsqrt(squares / model_width + EPS)[:, None]
    normed = (hidden_wide * inv_rms * norm_gain[None, :]).astype(jnp.bfloat16)
    received = dispatch(normed, None, targets, layout, first_local, held)
    gate_pre = jnp.einsum("secd,efd->secf", received, w_gate, preferred_element_type=jnp.float32)
    up_pre = jnp.einsum("secd,efd->secf", received, w_up, preferred_element_type=jnp.float32)
    sigma = jax.nn.sigmoid(gate_pre)
    active = (gate_pre * sigma * up_pre).astype(jnp.bfloat16)
    partial_value = jnp.einsum("secf,efd->secd", active, w_down, preferred_element_type=jnp.float32)
    mixed = combine(partial_value, scales, targets, layout, first_local, held)
    outcome = (hidden_wide + mixed).astype(jnp.bfloat16)
    logits = lax.psum(jnp.dot(outcome, head_weight, preferred_element_type=jnp.float32), "tp")
    classes = (labels[:, None] == jnp.arange(logits.shape[1], dtype=jnp.int32)[None, :]).astype(
        jnp.float32
    )
    totals = jnp.sum(jnp.exp(logits), axis=1, keepdims=True)
    token_loss = jnp.log(totals[:, 0]) - jnp.sum(logits * classes, axis=1)
    d_logits = (jnp.exp(logits) / totals - classes) * LOSS_SCALE
    d_outcome = jnp.dot(
        d_logits, head_weight.astype(jnp.float32).T, precision=lax.Precision.HIGHEST
    ) + grad_later.astype(jnp.float32)
    d_rounded = d_outcome.astype(jnp.bfloat16)
    grads_in = dispatch(d_rounded, scales, targets, layout, first_local, held)
    d_active = jnp.einsum("secd,efd->secf", grads_in, w_down, preferred_element_type=jnp.float32)
    grad_down = jnp.einsum(
        "secf,secd->efd", active, grads_in, preferred_element_type=jnp.float32
    ).astype(jnp.bfloat16)
    d_gate = (d_active * up_pre * sigma * (1.0 + gate_pre * (1.0 - sigma))).astype(jnp.bfloat16)
    d_up = (d_active * gate_pre * sigma).astype(jnp.bfloat16)
    grad_gate = jnp.einsum(
        "secf,secd->efd", d_gate, received, preferred_element_type=jnp.float32
    ).astype(jnp.bfloat16)
    grad_up = jnp.einsum(
        "secf,secd->efd", d_up, received, preferred_element_type=jnp.float32
    ).astype(jnp.bfloat16)
    d_partial = jnp.einsum(
        "secf,efd->secd", d_gate, w_gate, preferred_element_type=jnp.float32
    ) + jnp.einsum("secf,efd->secd", d_up, w_up, preferred_element_type=jnp.float32)
    d_normed = combine(d_partial, None, targets, layout, first_local, held)
    d_scaled = d_normed * norm_gain[None, :]
    slope = lax.psum(jnp.sum(d_scaled * hidden_wide, axis=1), "tp")[:, None] / model_width
    d_hidden = inv_rms * d_scaled - hidden_wide * (inv_rms * inv_rms * inv_rms) * slope
    grad_input = (d_outcome + d_hidden).astype(jnp.bfloat16)
    return (
        token_loss,
        outcome,
        grad_input,
        grad_gate.reshape(unit_rows, model_width),
        grad_up.reshape(unit_rows, model_width),
        grad_down.reshape(unit_rows, model_width),
    )


def solution(mesh):
    in_specs = (
        P("ep", "tp"),
        P("tp"),
        P("ep", None),
        P("ep", None),
        P("ep"),
        P("ep", "tp"),
        P("tp", None),
        P(("ep", "tp"), None),
        P(("ep", "tp"), None),
        P(("ep", "tp"), None),
    )
    out_specs = (
        P("ep"),
        P("ep", "tp"),
        P("ep", "tp"),
        P(("ep", "tp"), None),
        P(("ep", "tp"), None),
        P(("ep", "tp"), None),
    )
    return jax.shard_map(shards, mesh=mesh, in_specs=in_specs, out_specs=out_specs, check_vma=False)
```

profile of v0, /device:TPU:1, one launch (start us, length us, event | category | flops | bytes accessed | tf_op | source)
XLA Modules:
  0.0 645.8 jit_solution(3320304518517755561)
XLA Ops:
  9.3 9.5 %psum.21 = f32[128]{0:T(128)S(1)} all-reduce(f32[128]{0:T(128)S(1)} %fusion.49), channel_id=1, replica_groups=mesh['ep'=64,'tp'=4] {'tp'}, use_global_device_ids=true, to_apply=%region_4.5 | all-reduce | flops 128 | bytes 1024 | tf_op jit(solution)/shard_map/psum | solution.py:97
  20.7 11.2 %all_gather.6 = bf16[128,2048]{1,0:T(8,128)(2,1)S(1)} all-gather(bf16[128,512]{1,0:T(8,128)(2,1)S(1)} %fusion.51), channel_id=1, replica_groups=mesh['ep'=64,'tp'=4] {'tp'}, dimensions={1}, use_global_device_ids=true | all-gather | bytes 655360 | tf_op jit(solution)/shard_map/all_gather | solution.py:33
  32.8 10.3 %scatter_custom_fusion = bf16[1536,2048]{1,0:T(8,128)(2,1)} fusion(s32[1024]{0:T(1024)S(1)} %bitcast.102, bf16[]{:T(256)} %constant.75.clone.1, bf16[128,2048]{1,0:T(8,128)(2,1)S(1)} %all_gather.6), kind=kCustom, calls=%fused_computation.12 | custom fusion | bytes 6815746 | tf_op jit(solution)/shard_map/scatter | solution.py:28
  43.1 10.6 %reshape.329 = bf16[64,2,12,2048]{3,2,1,0:T(8,128)(2,1)} reshape(bf16[1536,2048]{1,0:T(8,128)(2,1)} %scatter_custom_fusion) | data formatting | bytes 12582912 | tf_op jit(solution)/shard_map/reshape | solution.py:36
  53.6 2.5 dynamic-slice_bitcast_fusion.1
  56.2 110.5 %all_to_all.20 = bf16[64,12,2048]{2,1,0:T(8,128)(2,1)S(1)} all-to-all(bf16[64,12,2048]{2,1,0:T(8,128)(2,1)S(1)} %dynamic-slice_bitcast_fusion.1), channel_id=1, replica_groups=mesh['ep'=64,'tp'=4] {'ep'}, dimensions={0} | all-to-all | bytes 6291456 | tf_op jit(solution)/shard_map/all_to_all | solution.py:40
  166.7 2.0 fusion.24
  169.2 3.2 multiply_convert_fusion.2
  174.2 3.7 copy.36
  178.0 7.3 %all-to-all-start.1 = ((bf16[64,12,2048]{2,1,0:T(8,128)(2,1)}), bf16[64,12,2048]{2,1,0:T(8,128)(2,1)}, u32[]{:S(2)}, u32[]{:S(2)}) async-start(bf16[64,12,2048]{2,1,0:T(8,128)(2,1)} %copy.36), calls=%async_computation.1 | async-start | bytes 8388608 | tf_op jit(solution)/shard_map/all_to_all | solution.py:49
  186.7 93.4 %all-to-all-done.1 = bf16[64,12,2048]{2,1,0:T(8,128)(2,1)} async-done(((bf16[64,12,2048]{2,1,0:T(8,128)(2,1)}), bf16[64,12,2048]{2,1,0:T(8,128)(2,1)}, u32[]{:S(2)}, u32[]{:S(2)}) %all-to-all-start.1) | async-done | bytes 3145760 | tf_op jit(solution)/shard_map/all_to_all | solution.py:49
  280.1 6.2 reshape.332
  286.3 11.1 %gather_fusion = bf16[1024,2048]{1,0:T(8,128)(2,1)} fusion(bf16[768,2048]{1,0:T(8,128)(2,1)} %reshape.332, s32[1024]{0:T(1024)S(1)} %broadcast_clamp_fusion), kind=kCustom, calls=%fused_computation | custom fusion | bytes 8392704 | tf_op jit(solution)/shard_map/gather | solution.py:60
  297.4 7.5 %fusion.1 = f32[128,2048]{1,0:T(8,128)} fusion(bf16[1024,2048]{1,0:T(8,128)(2,1)} %gather_fusion, f32[128,8]{1,0:T(8,128)S(1)} %broadcast_select_fusion), kind=kLoop, calls=%fused_computation.7 | loop fusion | flops 6029312 | bytes 5246976 | tf_op jit(solution)/shard_map/reduce_sum | solution.py:61
  305.1 20.6 %reduce-scatter.3.cloned.1.call-done = f32[128,512]{1,0:T(8,128)} async-done(((f32[128,2048]{1,0:T(8,128)}), f32[128,512]{1,0:T(8,128)}) %reduce-scatter.3.cloned.1.call-update) | async-done | bytes 262160 | tf_op jit(solution)/shard_map/reduce_scatter | solution.py:62
  326.9 6.6 %psum.22 = f32[128,4]{0,1:T(4,128)S(1)} all-reduce(f32[128,4]{0,1:T(4,128)S(1)} %fusion.75), channel_id=1, replica_groups=mesh['ep'=64,'tp'=4] {'tp'}, use_global_device_ids=true, to_apply=%region_8.9 | all-reduce | flops 512 | bytes 4096 | tf_op jit(solution)/shard_map/psum | solution.py:108
  334.6 9.9 %all_gather.7 = bf16[128,2048]{1,0:T(8,128)(2,1)S(1)} all-gather(bf16[128,512]{1,0:T(8,128)(2,1)S(1)} %get-tuple-element.18), channel_id=1, replica_groups=mesh['ep'=64,'tp'=4] {'tp'}, dimensions={1}, use_global_device_ids=true | all-gather | bytes 655360 | tf_op jit(solution)/shard_map/all_gather | solution.py:33
  344.6 10.8 %scatter_custom_fusion.1 = bf16[1536,2048]{1,0:T(8,128)(2,1)} fusion(s32[1024]{0:T(1024)S(1)} %bitcast.103, f32[128,2048]{1,0:T(8,128)S(1)} %convert_element_type.106, f32[1024]{0:T(1024)S(1)} %mul.175, bf16[]{:T(256)} %constant.75.clone.1), kind=kCustom, calls=%fused_computation.11 | custom fusion | flops 4194304 | bytes 7344130 | tf_op jit(solution)/shard_map/scatter | solution.py:28
  355.4 10.6 %reshape.333 = bf16[64,2,12,2048]{3,2,1,0:T(8,128)(2,1)} reshape(bf16[1536,2048]{1,0:T(8,128)(2,1)} %scatter_custom_fusion.1) | data formatting | bytes 12582912 | tf_op jit(solution)/shard_map/reshape | solution.py:36
  366.0 2.5 dynamic-slice_bitcast_fusion
  368.5 111.3 %all_to_all.21 = bf16[64,12,2048]{2,1,0:T(8,128)(2,1)S(1)} all-to-all(bf16[64,12,2048]{2,1,0:T(8,128)(2,1)S(1)} %dynamic-slice_bitcast_fusion), channel_id=1, replica_groups=mesh['ep'=64,'tp'=4] {'ep'}, dimensions={0} | all-to-all | bytes 6291456 | tf_op jit(solution)/shard_map/all_to_all | solution.py:40
  479.9 2.5 multiply_convert_fusion
  484.2 1.8 add_convert_fusion
  487.9 101.5 %all_to_all.22 = bf16[64,12,2048]{2,1,0:T(8,128)(2,1)} all-to-all(bf16[64,12,2048]{2,1,0:T(8,128)(2,1)S(1)} %copy.40), channel_id=1, replica_groups=mesh['ep'=64,'tp'=4] {'ep'}, dimensions={0} | all-to-all | bytes 6291456 | tf_op jit(solution)/shard_map/all_to_all | solution.py:49
  589.4 4.7 reshape.337
  594.1 6.2 gather_fusion.1
  600.4 7.6 %fusion = f32[128,2048]{1,0:T(8,128)} fusion(bf16[1024,2048]{1,0:T(8,128)(2,1)} %gather_fusion.1, f32[128,8]{1,0:T(8,128)} %get-tuple-element.8), kind=kLoop, calls=%fused_computation.5 | loop fusion | flops 6029312 | bytes 5246976 | tf_op jit(solution)/shard_map/reduce_sum | solution.py:61
  608.6 7.5 %bitcast_convert_fusion = bf16[384,2048]{1,0:T(8,128)(2,1)} fusion(bf16[64,12,2048]{2,1,0:T(8,128)(2,1)} %copy-done.4, bf16[64,1,12,384]{3,0,2,1:T(8,128)(2,1)S(1)} %copy-done.25), kind=kOutput, calls=%fused_computation.19 | convolution fusion | flops 1208745984 | bytes 5308416 | tf_op jit(solution)/shard_map/secf,secd->efd/dot_general | solution.py:121
  616.1 5.6 bitcast_convert_fusion.1
  621.7 5.3 bitcast_convert_fusion.2
  627.0 2.0 reduce-scatter.5.cloned.1.call-done
  630.1 6.6 %psum.23 = f32[128]{0:T(128)S(1)} all-reduce(f32[128]{0:T(128)S(1)} %fusion.57), channel_id=1, replica_groups=mesh['ep'=64,'tp'=4] {'tp'}, use_global_device_ids=true, to_apply=%region_15.16 | all-reduce | flops 128 | bytes 1024 | tf_op jit(solution)/shard_map/psum | solution.py:137
  (97 shorter events, 18.0 us)
Async XLA Ops:
  7.2 165.2 %copy-start = (bf16[384,2048]{1,0:T(8,128)(2,1)S(1)}, bf16[384,2048]{1,0:T(8,128)(2,1)}, u32[]{:S(2)}) copy-start(bf16[384,2048]{1,0:T(8,128)(2,1)} %param.19) | copy-start | bytes 4718596
  56.2 110.5 %copy-start.6 = (bf16[384,2048]{1,0:T(8,128)(2,1)S(1)}, bf16[384,2048]{1,0:T(8,128)(2,1)}, u32[]{:S(2)}) copy-start(bf16[384,2048]{1,0:T(8,128)(2,1)} %param.17) | copy-start | bytes 4718596
  166.7 2.0 copy-start.2
  166.7 2.5 copy-start.8
  169.2 3.2 copy-start.26
  172.4 5.6 copy-start.24
  178.0 7.8 %copy-start.18 = (f32[128,8]{0,1:T(8,128)S(1)}, f32[128,8]{0,1:T(8,128)}, u32[]{:S(2)}) copy-start(f32[128,8]{0,1:T(8,128)} %param.13) | copy-start | bytes 12292
  178.0 102.1 %all-to-all-start.1 = ((bf16[64,12,2048]{2,1,0:T(8,128)(2,1)}), bf16[64,12,2048]{2,1,0:T(8,128)(2,1)}, u32[]{:S(2)}, u32[]{:S(2)}) async-start(bf16[64,12,2048]{2,1,0:T(8,128)(2,1)} %copy.36), calls=%async_computation.1 | async-start | bytes 8388608 | tf_op jit(solution)/shard_map/all_to_all | solution.py:49
  185.3 140.5 %reduce-scatter.3.cloned.1.call-start = ((), (), s32[]{:S(2)}) async-start(), calls=%async_computation.6 | async-start | bytes 1310720 | tf_op jit(solution)/shard_map/reduce_scatter | solution.py:62
  297.4 28.3 %copy-start.5 = (bf16[128,512]{1,0:T(8,128)(2,1)S(1)}, bf16[128,512]{1,0:T(8,128)(2,1)}, u32[]{:S(2)}) copy-start(bf16[128,512]{1,0:T(8,128)(2,1)} %param.10) | copy-start | bytes 393220
  297.4 29.3 %copy-start.17 = (bf16[512,4]{0,1:T(4,128)(2,1)S(1)}, bf16[512,4]{0,1:T(4,128)(2,1)}, u32[]{:S(2)}) copy-start(bf16[512,4]{0,1:T(4,128)(2,1)} %param.16) | copy-start | bytes 12292
  297.4 36.1 %copy-start.19 = (s32[128]{0:T(128)S(1)}, s32[128]{0:T(128)}, u32[]{:S(2)}) copy-start(s32[128]{0:T(128)} %param.14) | copy-start | bytes 1540
  297.4 36.6 %copy-start.15 = (bf16[128,512]{1,0:T(8,128)(2,1)S(1)}, bf16[128,512]{1,0:T(8,128)(2,1)}, u32[]{:S(2)}) copy-start(bf16[128,512]{1,0:T(8,128)(2,1)} %param.15) | copy-start | bytes 393220
  305.0 324.1 %reduce-scatter.5.cloned.1.call-start = ((), (), s32[]{:S(2)}) async-start(), calls=%async_computation.7 | async-start | bytes 1310720 | tf_op jit(solution)/shard_map/reduce_scatter | solution.py:62
  326.7 7.3 %copy-start.14 = (bf16[128,512]{1,0:T(8,128)(2,1)}, bf16[128,512]{1,0:T(8,128)(2,1)S(1)}, u32[]{:S(2)}) copy-start(bf16[128,512]{1,0:T(8,128)(2,1)S(1)} %fusion.52) | copy-start | bytes 393220
  334.0 0.6 copy-start.20
  368.5 111.3 %copy-start.27 = (f32[64,1,12,384]{3,0,2,1:T(8,128)S(1)}, f32[64,1,12,384]{3,0,2,1:T(8,128)}, u32[]{:S(2)}) copy-start(f32[64,1,12,384]{3,0,2,1:T(8,128)} %copy-done.26) | copy-start | bytes 3538948
  368.5 111.3 %copy-start.28 = (f32[64,1,12,384]{3,0,2,1:T(8,128)S(1)}, f32[64,1,12,384]{3,0,2,1:T(8,128)}, u32[]{:S(2)}) copy-start(f32[64,1,12,384]{3,0,2,1:T(8,128)} %get-tuple-element.17) | copy-start | bytes 3538948
  479.8 2.5 copy-start.4
  479.9 2.6 copy-start.7
  482.3 1.9 copy-start.10
  482.4 1.9 copy-start.12
  482.4 1.8 copy-start.9
  600.3 7.7 %copy-start.21 = (f32[128]{0:T(128)S(1)}, f32[128]{0:T(128)}, u32[]{:S(2)}) copy-start(f32[128]{0:T(128)} %copy-done.20) | copy-start | bytes 1540
  600.4 7.7 %copy-start.22 = (f32[128]{0:T(128)S(1)}, f32[128]{0:T(128)}, u32[]{:S(2)}) copy-start(f32[128]{0:T(128)} %get-tuple-element.7) | copy-start | bytes 1540
  600.4 8.2 %copy-start.25 = (bf16[64,1,12,384]{3,0,2,1:T(8,128)(2,1)S(1)}, bf16[64,1,12,384]{3,0,2,1:T(8,128)(2,1)}, u32[]{:S(2)}) copy-start(bf16[64,1,12,384]{3,0,2,1:T(8,128)(2,1)} %copy-done.24) | copy-start | bytes 1769476
  608.5 7.5 %copy-start.3 = (bf16[64,12,2048]{2,1,0:T(8,128)(2,1)S(1)}, bf16[64,12,2048]{2,1,0:T(8,128)(2,1)}, u32[]{:S(2)}) copy-start(bf16[64,12,2048]{2,1,0:T(8,128)(2,1)} %copy-done.2) | copy-start | bytes 9437188
  608.6 7.5 %copy-start.13 = (bf16[64,1,12,384]{3,0,2,1:T(8,128)(2,1)S(1)}, bf16[64,1,12,384]{3,0,2,1:T(8,128)(2,1)}, u32[]{:S(2)}) copy-start(bf16[64,1,12,384]{3,0,2,1:T(8,128)(2,1)} %copy-done.12) | copy-start | bytes 1769476
  616.1 5.6 copy-start.11
  621.7 7.3 %copy-start.16 = (f32[512]{0:T(512)S(1)}, f32[512]{0:T(512)}, u32[]{:S(2)}) copy-start(f32[512]{0:T(512)} %param.11) | copy-start | bytes 6148
  621.7 15.1 %copy-start.23 = (f32[128]{0:T(128)S(1)}, f32[128]{0:T(128)}, u32[]{:S(2)}) copy-start(f32[128]{0:T(128)} %get-tuple-element.14) | copy-start | bytes 1540
  621.7 16.8 %copy-start.1 = (bf16[384,2048]{1,0:T(8,128)(2,1)S(1)}, bf16[384,2048]{1,0:T(8,128)(2,1)}, u32[]{:S(2)}) copy-start(bf16[384,2048]{1,0:T(8,128)(2,1)} %param.19) | copy-start | bytes 4718596
Sparse Core Ops, SparseCore 0:
  305.1 20.6 reduce-scatter.2
  608.1 20.8 reduce-scatter.4
where the time goes:
time: 656 us; the launch traced here: 646 us
  blocking collectives  367 us (56%)
  waiting for transfers between devices  116 us (18%)
  local copies, waits for them, and re-layouts  72.8 us (11%)
  other arithmetic  35 us (5%)
  matrix products  32 us (5%)
  between operations  14.9 us (2%)
  starting transfers between devices  7.78 us (1%)
    all_to_all x2, blocking collectives, dispatch(): lax.all_to_all(outgoing, 'ep', split_axis=0, concat_axis=0, tiled=True)  222 us
    all_to_all x1, blocking collectives, combine(): lax.all_to_all(outgoing, 'ep', split_axis=0, concat_axis=0, tiled=True)  102 us
    all_to_all x1, waiting for transfers between devices, combine(): lax.all_to_all(outgoing, 'ep', split_axis=0, concat_axis=0, tiled=True)  93.4 us
    reduce_scatter x2, waiting for transfers between devices, combine(): return lax.psum_scatter(summed, 'tp', scatter_dimension=1, tiled=True)  22.7 us
    reshape x2, local copies, waits for them, and re-layouts, dispatch(): filled = filled.reshape(dev_count, local_count, capacity, width)  21.2 us
    all_gather x2, blocking collectives, dispatch(): whole_rows = lax.all_gather(token_rows, 'tp', axis=1, tiled=True)  21.1 us
    gather x2, local copies, waits for them, and re-layouts, combine(): picked = flat_rows[rows].astype(jnp.float32) * factor[:, None]  17.3 us
    reduce_sum x2, other arithmetic, combine(): summed = jnp.sum(picked.reshape(tok_count, top_count, width), axis=1)  15.1 us
  transfers between devices with their start and end apart: 3, of which 3 were waited for; matrix products, arithmetic and copies ran while one was open for 3% of the time, Pallas kernels for 0%

commit v1 on v0

v1 whole, which is shorter than its diff:
```python
import functools

import jax
import jax.numpy as jnp
from jax import lax
from jax.experimental import pallas as pl
from jax.experimental.pallas import tpu as pltpu
from jax.sharding import PartitionSpec as P

FF = 768
EPS = 1e-06
LOSS_SCALE = 64.0
CAP = 12
LABELS = 4
QUAD = 4
LANES = 128
MESH = pl.DeviceIdType.MESH
F32 = jnp.float32
BF16 = jnp.bfloat16


def place(nj):
    ep = lax.axis_index("ep")
    t = lax.axis_index("tp")
    z = lax.div(ep, nj)
    j = lax.rem(ep, nj)
    return z, j, t


def z_order(nz):
    half = nz // 2
    order = []
    for back in range(half + 1):
        for k in (half - back, half + back):
            if 0 < k < nz and k not in order:
                order.append(k)
    return order


def rcopy(src, dst, send, recv, device):
    return pltpu.make_async_remote_copy(
        src_ref=src, dst_ref=dst, send_sem=send, recv_sem=recv, device_id=device, device_id_type=MESH
    )


def later(*args):
    return lambda: rcopy(*args)


def local_copy(*args):
    return lambda: pltpu.make_async_copy(*args)


def enter(nz, nj):
    z, j, t = place(nj)
    barrier = pltpu.get_barrier_semaphore()
    for k in range(1, nz):
        pl.semaphore_signal(
            barrier, inc=1, device_id={"ep": lax.rem(z + k, nz) * nj + j}, device_id_type=MESH
        )
    for k in range(1, nj):
        pl.semaphore_signal(
            barrier, inc=1, device_id={"ep": z * nj + lax.rem(j + k, nj)}, device_id_type=MESH
        )
    for k in range(1, 4):
        pl.semaphore_signal(barrier, inc=1, device_id={"tp": lax.rem(t + k, 4)}, device_id_type=MESH)
    pl.semaphore_wait(barrier, nz - 1 + nj - 1 + 3)


def column(t, f, chunks):
    return pl.ds(pl.multiple_of((t * chunks + f) * LANES, LANES), LANES)


def expert_keys(meta, z, ne):
    toks = meta.shape[1]
    names = (lax.broadcasted_iota(jnp.int32, (ne, toks), 0) + z * ne).astype(F32)
    named = jnp.zeros((ne, toks), F32)
    weight = jnp.zeros((ne, toks), F32)
    for k in range(8):
        hit = meta[k : k + 1, :] == names
        named = jnp.where(hit, 1.0, named)
        weight = jnp.where(hit, meta[8 + k : 9 + k, :], weight)
    earlier = (
        lax.broadcasted_iota(jnp.int32, (toks, toks), 0) < lax.broadcasted_iota(jnp.int32, (toks, toks), 1)
    ).astype(F32)
    rank = jnp.dot(named.astype(BF16), earlier.astype(BF16), preferred_element_type=F32)
    return jnp.where(named > 0.0, rank, -64.0), weight


def split(value):
    high = value.astype(BF16)
    return high, (value - high.astype(F32)).astype(BF16)


def build_pick(meta_ref, z, nz, ne, pick_hi, pick_lo):
    for zz in range(nz):
        q, zq = zz // QUAD, zz % QUAD
        key, weight = expert_keys(meta_ref[zz], z, ne)
        key = key + float(CAP * zq)
        row = lax.broadcasted_iota(jnp.int32, (ne, QUAD * CAP, LANES), 1).astype(F32)
        at = row == key[:, None, :]
        where = slice(zq * LANES, (zq + 1) * LANES)
        if pick_lo is None:
            one = jnp.where(at, 1.0, 0.0).astype(BF16)
            pick_hi[q, :, where] = one.reshape(ne * QUAD * CAP, LANES)
        else:
            high, low = split(jnp.where(at, weight[:, None, :], 0.0))
            pick_hi[q, :, where] = high.reshape(ne * QUAD * CAP, LANES)
            pick_lo[q, :, where] = low.reshape(ne * QUAD * CAP, LANES)


def build_place(meta_ref, z, nz, ne, place_hi, place_lo):
    wide = ne * QUAD * CAP
    expert = lax.broadcasted_iota(jnp.int32, (ne, wide), 0).astype(F32)
    lane = lax.broadcasted_iota(jnp.int32, (ne, wide), 1).astype(F32)
    start = expert * float(QUAD * CAP)
    spread = jnp.where((lane >= start) & (lane < start + float(QUAD * CAP)), 1.0, 0.0)
    base = jnp.sum(spread * start, axis=0, keepdims=True)
    within = lane[0:1] - base
    spread = spread.astype(BF16)
    for zz in range(nz):
        q, zq = zz // QUAD, zz % QUAD
        key, weight = expert_keys(meta_ref[zz], z, ne)
        key = key + float(CAP * zq)
        high, low = split(weight)
        fill = jnp.zeros((LANES - 3 * ne, LANES), F32)
        stack = jnp.concatenate([key, high.astype(F32), low.astype(F32), fill], axis=0)
        turned = jnp.transpose(stack).astype(BF16)
        keys = jnp.dot(turned[:, 0:ne], spread, preferred_element_type=F32)
        at = keys == within
        where = slice(zq * LANES, (zq + 1) * LANES)
        if place_lo is None:
            place_hi[q, where, :] = jnp.where(at, 1.0, 0.0).astype(BF16)
        else:
            highs = jnp.dot(turned[:, ne : 2 * ne], spread, preferred_element_type=F32)
            lows = jnp.dot(turned[:, 2 * ne : 3 * ne], spread, preferred_element_type=F32)
            place_hi[q, where, :] = jnp.where(at, highs, 0.0).astype(BF16)
            place_lo[q, where, :] = jnp.where(at, lows, 0.0).astype(BF16)


class Exchange:
    def __init__(self, nj, buf, send, recv):
        self.t = lax.axis_index("tp")
        self.buf, self.send, self.recv = buf, send, recv

    def copies(self):
        t = self.t
        for k in range(1, 4):
            to = lax.rem(t + k, 4)
            yield later(
                self.buf.at[t], self.buf.at[t], self.send.at[k], self.recv.at[t], {"tp": to}
            ), later(self.buf.at[t], self.buf.at[to], self.send.at[k], self.recv.at[to], {"tp": to})

    def start(self, value):
        self.buf[self.t] = value
        for out, _ in self.copies():
            out().start()

    def total(self):
        for _, arriving in self.copies():
            arriving().wait_recv()
        return (self.buf[0] + self.buf[1]) + (self.buf[2] + self.buf[3])

    def drain(self):
        for out, _ in self.copies():
            out().wait_send()


def to_row(col):
    return jnp.transpose(jnp.broadcast_to(col, (LANES, LANES)))[0:8, :]


def to_columns(row):
    return jnp.transpose(jnp.broadcast_to(row, (LANES, LANES)))


class Dispatch:
    def __init__(self, nz, nj, chunks, pick_hi, pick_lo, out, scratch):
        self.nz, self.nj, self.chunks = nz, nj, chunks
        self.z, self.j, self.t = place(nj)
        self.pick_hi, self.pick_lo, self.out = pick_hi, pick_lo, out
        (self.zbuf, self.xsend, self.xrecv, self.zss, self.zrs, self.xss, self.xrs, self.xl,
         self.yss, self.yrs, self.yl) = scratch

    @staticmethod
    def scratch(nz, nj, chunks):
        rows = nz * CAP
        return [
            pltpu.VMEM((chunks, nz, LANES, LANES), BF16),
            pltpu.VMEM((chunks, nj, 2, rows, LANES), BF16),
            pltpu.VMEM((chunks, 2, nj, rows, LANES), BF16),
            pltpu.SemaphoreType.DMA((chunks, nz)),
            pltpu.SemaphoreType.DMA((chunks, nz)),
            pltpu.SemaphoreType.DMA((chunks, nj)),
            pltpu.SemaphoreType.DMA((chunks, nj)),
            pltpu.SemaphoreType.DMA((chunks,)),
            pltpu.SemaphoreType.DMA((chunks, 3)),
            pltpu.SemaphoreType.DMA((chunks, 3)),
            pltpu.SemaphoreType.DMA((chunks,)),
        ]

    def z_copies(self, f):
        z, j, nz, nj = self.z, self.j, self.nz, self.nj
        for k in z_order(nz):
            to = lax.rem(z + k, nz)
            device = {"ep": to * nj + j}
            mine = self.zbuf.at[f, z]
            yield later(mine, mine, self.zss.at[f, k], self.zrs.at[f, z], device), later(
                mine, self.zbuf.at[f, to], self.zss.at[f, k], self.zrs.at[f, to], device
            )

    def z_send(self, f, value):
        self.zbuf[f, self.z] = value
        for out, _ in self.z_copies(f):
            out().start()

    def pick(self, f):
        for _, arriving in self.z_copies(f):
            arriving().wait_recv()
        nj, rows = self.nj, QUAD * CAP
        for q in range(self.nz // QUAD):
            block = self.zbuf[f, q * QUAD : (q + 1) * QUAD].reshape(QUAD * LANES, LANES)
            got = jnp.dot(self.pick_hi[q], block, preferred_element_type=F32)
            if self.pick_lo is not None:
                got = got + jnp.dot(self.pick_lo[q], block, preferred_element_type=F32)
            self.xsend[f, :, :, q * rows : (q + 1) * rows, :] = got.astype(BF16).reshape(nj, 2, rows, LANES)

    def x_copies(self, f):
        z, j, nj = self.z, self.j, self.nj
        for k in range(1, nj):
            to = lax.rem(j + k, nj)
            device = {"ep": z * nj + to}
            yield later(
                self.xsend.at[f, to], self.xrecv.at[f, :, j], self.xss.at[f, k], self.xrs.at[f, j], device
            ), later(
                self.xsend.at[f, to], self.xrecv.at[f, :, to], self.xss.at[f, k], self.xrs.at[f, to], device
            )

    def x_local(self, f):
        return local_copy(self.xsend.at[f, self.j], self.xrecv.at[f, :, self.j], self.xl.at[f])

    def x_send(self, f):
        for out, _ in self.x_copies(f):
            out().start()
        self.x_local(f)().start()

    def x_wait(self, f):
        for _, arriving in self.x_copies(f):
            arriving().wait_recv()
        self.x_local(f)().wait()

    def y_copies(self, f):
        t = self.t
        half = lax.div(t, 2)
        mate = t + 1 - 2 * lax.rem(t, 2)
        across = 3 - t
        mine, theirs = self.out.at[:, :, column(t, f, self.chunks)], self.out.at[:, :, column(across, f, self.chunks)]
        far = self.out.at[:, :, column(3 - mate, f, self.chunks)]
        near = self.out.at[:, :, column(mate, f, self.chunks)]
        src = self.xrecv.at[f, half]
        other = self.xrecv.at[f, 1 - half]
        sends = (
            later(src, mine, self.yss.at[f, 0], self.yrs.at[f, 0], {"tp": mate}),
            later(other, mine, self.yss.at[f, 1], self.yrs.at[f, 1], {"tp": across}),
            later(theirs, theirs, self.yss.at[f, 2], self.yrs.at[f, 2], {"tp": mate}),
        )
        arrivals = (
            later(src, near, self.yss.at[f, 0], self.yrs.at[f, 0], {"tp": mate}),
            later(src, theirs, self.yss.at[f, 1], self.yrs.at[f, 1], {"tp": across}),
            later(src, far, self.yss.at[f, 2], self.yrs.at[f, 2], {"tp": mate}),
        )
        return sends, arrivals, local_copy(src, mine, self.yl.at[f])

    def y_send(self, f):
        sends, _, local = self.y_copies(f)
        sends[1]().start()
        sends[0]().start()
        local().start()

    def y_forward(self, f):
        sends, arrivals, _ = self.y_copies(f)
        arrivals[1]().wait_recv()
        sends[2]().start()

    def run(self):
        n = self.chunks
        for step in range(n + 2):
            if step < n:
                self.pick(step)
                self.x_send(step)
            if 0 <= step - 1 < n:
                self.x_wait(step - 1)
                self.y_send(step - 1)
            if 0 <= step - 2 < n:
                self.y_forward(step - 2)
        for f in range(n):
            _, arrivals, local = self.y_copies(f)
            arrivals[0]().wait_recv()
            arrivals[2]().wait_recv()
            local().wait()

    def drain(self):
        for f in range(self.chunks):
            for out, _ in self.z_copies(f):
                out().wait_send()
            for out, _ in self.x_copies(f):
                out().wait_send()
            for out in self.y_copies(f)[0]:
                out().wait_send()


class Combine:
    def __init__(self, nz, nj, chunks, value, place_hi, place_lo, scratch):
        self.nz, self.nj, self.chunks, self.value = nz, nj, chunks, value
        self.z, self.j, self.t = place(nj)
        self.place_hi, self.place_lo = place_hi, place_lo
        (self.yr, self.ysum, self.xs, self.xr, self.zs, self.zr, self.yss, self.yrs,
         self.xss, self.xrs, self.xl, self.zss, self.zrs) = scratch

    @staticmethod
    def scratch(nz, nj, chunks):
        rows = nz * CAP
        return [
            pltpu.VMEM((chunks, 2, nj, rows, LANES), BF16),
            pltpu.VMEM((chunks, nj, rows, LANES), BF16),
            pltpu.VMEM((chunks, 2, nj, rows, LANES), BF16),
            pltpu.VMEM((chunks, nj, 2, rows, LANES), BF16),
            pltpu.VMEM((chunks, nz, LANES, LANES), BF16),
            pltpu.VMEM((chunks, nz, LANES, LANES), BF16),
            pltpu.SemaphoreType.DMA((chunks, 3)),
            pltpu.SemaphoreType.DMA((chunks, 3)),
            pltpu.SemaphoreType.DMA((chunks, nj)),
            pltpu.SemaphoreType.DMA((chunks, nj)),
            pltpu.SemaphoreType.DMA((chunks,)),
            pltpu.SemaphoreType.DMA((chunks, nz)),
            pltpu.SemaphoreType.DMA((chunks, nz)),
        ]

    def y_copies(self, f):
        t = self.t
        half = lax.div(t, 2)
        mate = t + 1 - 2 * lax.rem(t, 2)
        across = 3 - t
        sends = (
            later(self.value.at[:, :, column(mate, f, self.chunks)], self.yr.at[f, 0], self.yss.at[f, 0],
                  self.yrs.at[f, 0], {"tp": mate}),
            later(self.value.at[:, :, column(3 - mate, f, self.chunks)], self.yr.at[f, 1], self.yss.at[f, 1],
                  self.yrs.at[f, 1], {"tp": mate}),
            later(self.ysum.at[f], self.xs.at[f, half], self.yss.at[f, 2], self.yrs.at[f, 2],
                  {"tp": across}),
        )
        last = later(self.ysum.at[f], self.xs.at[f, 1 - half], self.yss.at[f, 2], self.yrs.at[f, 2],
                     {"tp": across})
        return sends, (sends[0], sends[1], last)

    def start(self):
        for f in range(self.chunks):
            sends, _ = self.y_copies(f)
            sends[1]().start()
            sends[0]().start()

    def y_sum(self, f):
        t = self.t
        sends, arrivals = self.y_copies(f)
        arrivals[1]().wait_recv()
        for i in range(self.nj):
            own = self.value[i, :, column(3 - t, f, self.chunks)].astype(F32)
            self.ysum[f, i] = (own + self.yr[f, 1, i].astype(F32)).astype(BF16)
        sends[2]().start()
        arrivals[0]().wait_recv()
        half = lax.div(t, 2)
        for i in range(self.nj):
            own = self.value[i, :, column(t, f, self.chunks)].astype(F32)
            self.xs[f, half, i] = (own + self.yr[f, 0, i].astype(F32)).astype(BF16)

    def x_copies(self, f):
        z, j, nj = self.z, self.j, self.nj
        for k in range(1, nj):
            to = lax.rem(j + k, nj)
            device = {"ep": z * nj + to}
            yield later(
                self.xs.at[f, :, to], self.xr.at[f, j], self.xss.at[f, k], self.xrs.at[f, j], device
            ), later(
                self.xs.at[f, :, to], self.xr.at[f, to], self.xss.at[f, k], self.xrs.at[f, to], device
            )

    def x_local(self, f):
        return local_copy(self.xs.at[f, :, self.j], self.xr.at[f, self.j], self.xl.at[f])

    def x_send(self, f):
        self.y_copies(f)[1][2]().wait_recv()
        for out, _ in self.x_copies(f):
            out().start()
        self.x_local(f)().start()

    def z_copies(self, f):
        z, j, nz, nj = self.z, self.j, self.nz, self.nj
        for k in z_order(nz):
            to = lax.rem(z + k, nz)
            device = {"ep": to * nj + j}
            yield later(
                self.zs.at[f, to], self.zr.at[f, z], self.zss.at[f, k], self.zrs.at[f, z], device
            ), later(
                self.zs.at[f, to], self.zr.at[f, to], self.zss.at[f, k], self.zrs.at[f, to], device
            )

    def mix(self, f):
        for _, arriving in self.x_copies(f):
            arriving().wait_recv()
        self.x_local(f)().wait()
        rows = QUAD * CAP
        for q in range(self.nz // QUAD):
            got = self.xr[f, :, :, q * rows : (q + 1) * rows, :].reshape(self.nj * 2 * rows, LANES)
            part = jnp.dot(self.place_hi[q], got, preferred_element_type=F32)
            if self.place_lo is not None:
                part = part + jnp.dot(self.place_lo[q], got, preferred_element_type=F32)
            self.zs[f, q * QUAD : (q + 1) * QUAD] = part.astype(BF16).reshape(QUAD, LANES, LANES)
        for out, _ in self.z_copies(f):
            out().start()

    def run(self):
        n = self.chunks
        for step in range(n + 2):
            if step < n:
                self.y_sum(step)
            if 0 <= step - 1 < n:
                self.x_send(step - 1)
            if 0 <= step - 2 < n:
                self.mix(step - 2)

    def result(self, f):
        for _, arriving in self.z_copies(f):
            arriving().wait_recv()
        total = self.zs[f, self.z].astype(F32)
        for k in range(1, self.nz):
            total = total + self.zr[f, lax.rem(self.z + k, self.nz)].astype(F32)
        return total

    def drain(self):
        for f in range(self.chunks):
            for out in self.y_copies(f)[0]:
                out().wait_send()
            for out, _ in self.x_copies(f):
                out().wait_send()
            for out, _ in self.z_copies(f):
                out().wait_send()


def lanes(f):
    return slice(f * LANES, (f + 1) * LANES)


def first_kernel(nz, nj, chunks, hidden_ref, gain_ref, own_ref, out_ref, meta_ref, inv_ref,
                 pick_ref, sum_buf, sum_ss, sum_rs, meta_ss, meta_rs, *scratch):
    z, j, t = place(nj)
    enter(nz, nj)
    squares = Exchange(nj, sum_buf, sum_ss, sum_rs)
    wide = hidden_ref[...].astype(F32)
    squares.start(to_row(jnp.sum(wide * wide, axis=1, keepdims=True)))

    def meta_copies():
        for k in range(1, nz):
            to = lax.rem(z + k, nz)
            device = {"ep": to * nj + j}
            yield later(own_ref, meta_ref.at[z], meta_ss.at[k], meta_rs.at[z], device), later(
                own_ref, meta_ref.at[to], meta_ss.at[k], meta_rs.at[to], device
            )

    for out, _ in meta_copies():
        out().start()
    meta_ref[z] = own_ref[...]
    move = Dispatch(nz, nj, chunks, pick_ref, None, out_ref, scratch)
    total = to_columns(squares.total()[0:1, :])
    inv = lax.rsqrt(total / (4 * chunks * LANES) + EPS)
    inv_ref[...] = inv
    for f in range(chunks):
        normed = hidden_ref[:, lanes(f)].astype(F32) * inv * gain_ref[0:1, lanes(f)]
        move.z_send(f, normed.astype(BF16))
    for _, arriving in meta_copies():
        arriving().wait_recv()
    build_pick(meta_ref, z, nz, 2 * nj, pick_ref, None)
    move.run()
    move.drain()
    squares.drain()
    for out, _ in meta_copies():
        out().wait_send()


def middle_kernel(nz, nj, chunks, value_ref, meta_ref, hidden_ref, later_ref, head_ref, labels_ref,
                  outcome_ref, loss_ref, dout_ref, grads_ref,
                  place_hi, place_lo, pick_hi, pick_lo, sum_buf, sum_ss, sum_rs, *scratch):
    z, j, t = place(nj)
    enter(nz, nj)
    cut = len(Combine.scratch(nz, nj, chunks))
    back = Combine(nz, nj, chunks, value_ref, place_hi, place_lo, scratch[:cut])
    back.start()
    build_place(meta_ref, z, nz, 2 * nj, place_hi, place_lo)
    build_pick(meta_ref, z, nz, 2 * nj, pick_hi, pick_lo)
    back.run()
    logits = jnp.zeros((8, LANES), F32)
    for f in range(chunks):
        mixed = back.result(f)
        outcome = (hidden_ref[:, lanes(f)].astype(F32) + mixed).astype(BF16)
        outcome_ref[:, lanes(f)] = outcome
        logits = logits + lax.dot_general(
            head_ref[:, lanes(f)], outcome, (((1,), (1,)), ((), ())), preferred_element_type=F32
        )
    sums = Exchange(nj, sum_buf, sum_ss, sum_rs)
    sums.start(logits)
    logits = sums.total()
    row = lax.broadcasted_iota(jnp.int32, (8, LANES), 0)
    live = row < LABELS
    hot = jnp.where(row == labels_ref[0:1, :], 1.0, 0.0)
    powers = jnp.where(live, jnp.exp(jnp.where(live, logits, 0.0)), 0.0)
    totals = jnp.sum(powers, axis=0, keepdims=True)
    loss = jnp.log(totals) - jnp.sum(logits * hot, axis=0, keepdims=True)
    loss_ref[...] = jnp.broadcast_to(loss, (8, LANES))
    d_logits = (powers / totals - hot) * LOSS_SCALE
    d_logits = jnp.concatenate([d_logits, jnp.zeros((LANES - 8, LANES), F32)], axis=0)
    d_logits = jnp.transpose(d_logits)
    move = Dispatch(nz, nj, chunks, pick_hi, pick_lo, grads_ref, scratch[cut:])
    for f in range(chunks):
        d_outcome = later_ref[:, lanes(f)].astype(F32)
        term = jnp.zeros((LANES, LANES), F32)
        for label in range(LABELS):
            weight = head_ref[label : label + 1, lanes(f)].astype(F32)
            term = term + d_logits[:, label : label + 1] * weight
        d_outcome = term + d_outcome
        dout_ref[:, lanes(f)] = d_outcome
        move.z_send(f, d_outcome.astype(BF16))
    move.run()
    move.drain()
    sums.drain()
    back.drain()


def last_kernel(nz, nj, chunks, value_ref, meta_ref, hidden_ref, gain_ref, inv_ref, dout_ref,
                grad_ref, place_ref, scaled_ref, sum_buf, sum_ss, sum_rs, *scratch):
    z, j, t = place(nj)
    enter(nz, nj)
    back = Combine(nz, nj, chunks, value_ref, place_ref, None, scratch)
    back.start()
    build_place(meta_ref, z, nz, 2 * nj, place_ref, None)
    back.run()
    slope = jnp.zeros((LANES, LANES), F32)
    for f in range(chunks):
        scaled = back.result(f) * gain_ref[0:1, lanes(f)]
        scaled_ref[:, lanes(f)] = scaled
        slope = slope + scaled * hidden_ref[:, lanes(f)].astype(F32)
    sums = Exchange(nj, sum_buf, sum_ss, sum_rs)
    sums.start(to_row(jnp.sum(slope, axis=1, keepdims=True)))
    slope = to_columns(sums.total()[0:1, :]) / (4 * chunks * LANES)
    inv = inv_ref[...]
    cube = inv * inv * inv
    for f in range(chunks):
        d_hidden = inv * scaled_ref[:, lanes(f)] - hidden_ref[:, lanes(f)].astype(F32) * cube * slope
        grad_ref[:, lanes(f)] = (dout_ref[:, lanes(f)] + d_hidden).astype(BF16)
    sums.drain()
    back.drain()


def shards(nz, nj, hidden_in, norm_gain, expert_ids, routing_weight, labels, grad_later, head_weight,
           gate_weight, up_weight, down_weight):
    width = gate_weight.shape[1]
    chunks = hidden_in.shape[1] // LANES
    ne = 2 * nj
    nq = nz // QUAD
    rows = nz * CAP
    high = ne * QUAD * CAP
    tall = QUAD * LANES
    vmem = pl.BlockSpec(memory_space=pltpu.VMEM)
    sems = [pltpu.SemaphoreType.DMA((4,)), pltpu.SemaphoreType.DMA((4,))]
    sums = [pltpu.VMEM((4, 8, LANES), F32)] + sems

    def call(kernel, name, ident, outs, scratch, *args):
        return pl.pallas_call(
            functools.partial(kernel, nz, nj, chunks),
            out_shape=outs,
            in_specs=[vmem] * len(args),
            out_specs=[vmem] * len(outs),
            scratch_shapes=scratch,
            name=name,
            compiler_params=pltpu.CompilerParams(collective_id=ident, has_side_effects=True),
        )(*args)

    buffer = jax.ShapeDtypeStruct((nj, rows, width), BF16)
    own = jnp.concatenate([expert_ids.T.astype(F32), routing_weight.T], axis=0)
    gain = norm_gain[None, :]
    head = jnp.concatenate([head_weight.T, jnp.zeros_like(head_weight.T)], axis=0)
    received, meta, inv = call(
        first_kernel, "dispatch_tokens", 1,
        [buffer, jax.ShapeDtypeStruct((nz, 16, LANES), F32), jax.ShapeDtypeStruct((LANES, LANES), F32)],
        [pltpu.VMEM((nq, high, tall), BF16)] + sums
        + [pltpu.SemaphoreType.DMA((nz,)), pltpu.SemaphoreType.DMA((nz,))]
        + Dispatch.scratch(nz, nj, chunks),
        hidden_in, gain, own,
    )
    received = received.reshape(nj * rows, width)

    def dot(a, b, ca, cb):
        return lax.dot_general(a, b, (((ca,), (cb,)), ((), ())), preferred_element_type=F32)

    gate_pre = dot(received, gate_weight, 1, 1)
    up_pre = dot(received, up_weight, 1, 1)
    sigma = jax.nn.sigmoid(gate_pre)
    active = (gate_pre * sigma * up_pre).astype(BF16)
    partial_value = dot(active, down_weight, 1, 0).astype(BF16)
    outcome, loss, d_outcome, grads_in = call(
        middle_kernel, "combine_head_dispatch", 2,
        [
            jax.ShapeDtypeStruct(hidden_in.shape, BF16),
            jax.ShapeDtypeStruct((8, LANES), F32),
            jax.ShapeDtypeStruct(hidden_in.shape, F32),
            buffer,
        ],
        [pltpu.VMEM((nq, tall, high), BF16)] * 2 + [pltpu.VMEM((nq, high, tall), BF16)] * 2 + sums
        + Combine.scratch(nz, nj, chunks) + Dispatch.scratch(nz, nj, chunks),
        partial_value.reshape(nj, rows, width), meta, hidden_in, grad_later, head, labels[None, :],
    )
    grads_in = grads_in.reshape(nj * rows, width)
    d_active = dot(grads_in, down_weight, 1, 1)
    d_gate = (d_active * up_pre * sigma * (1.0 + gate_pre * (1.0 - sigma))).astype(BF16)
    d_up = (d_active * gate_pre * sigma).astype(BF16)
    d_partial = (dot(d_gate, gate_weight, 1, 0) + dot(d_up, up_weight, 1, 0)).astype(BF16)
    grad_down = dot(active, grads_in, 0, 0).astype(BF16)
    grad_gate = dot(d_gate, received, 0, 0).astype(BF16)
    grad_up = dot(d_up, received, 0, 0).astype(BF16)
    (grad_input,) = call(
        last_kernel, "combine_grad", 3,
        [jax.ShapeDtypeStruct(hidden_in.shape, BF16)],
        [pltpu.VMEM((nq, tall, high), BF16), pltpu.VMEM(hidden_in.shape, F32)] + sums
        + Combine.scratch(nz, nj, chunks),
        d_partial.reshape(nj, rows, width), meta, hidden_in, gain, inv, d_outcome,
    )
    return loss[0], outcome, grad_input, grad_gate, grad_up, grad_down


def solution(mesh, nj=8):
    nz = mesh.shape["ep"] // nj
    in_specs = (
        P("ep", "tp"),
        P("tp"),
        P("ep", None),
        P("ep", None),
        P("ep"),
        P("ep", "tp"),
        P("tp", None),
        P(("ep", "tp"), None),
        P(("ep", "tp"), None),
        P(("ep", "tp"), None),
    )
    out_specs = (
        P("ep"),
        P("ep", "tp"),
        P("ep", "tp"),
        P(("ep", "tp"), None),
        P(("ep", "tp"), None),
        P(("ep", "tp"), None),
    )
    return jax.shard_map(
        functools.partial(shards, nz, nj), mesh=mesh, in_specs=in_specs, out_specs=out_specs, check_vma=False
    )
```

time: 656 us -> 297 us (0.45); the launches traced: 646 us -> 297 us
  blocking collectives: 367 us -> 0 us
  Pallas kernels: 0 us -> 261 us
  waiting for transfers between devices: 116 us -> 0 us
  local copies, waits for them, and re-layouts: 72.8 us -> 4.75 us
  other arithmetic: 35 us -> 2.09 us
  between operations: 14.9 us -> 0.75 us
  starting transfers between devices: 7.78 us -> 0 us
    all_to_all x3 -> x0, blocking collectives: 323 us -> none  [the longest x2 222 us: dispatch(): lax.all_to_all(outgoing, 'ep', split_axis=0, concat_axis=0, tiled=True)]
    pallas_call x0 -> x3, Pallas kernels: none -> 261 us  [call(): pl.pallas_call(functools.partial(kernel, nz, nj, chunks), out_shape=outs,...]
    all_to_all x1 -> x0, waiting for transfers between devices: 93.4 us -> none  [combine(): lax.all_to_all(outgoing, 'ep', split_axis=0, concat_axis=0, tiled=True)]
    reshape x6 -> x0, local copies, waits for them, and re-layouts: 37.1 us -> none  [the longest x2 21.2 us: dispatch(): filled = filled.reshape(dev_count, local_count, capacity, width)]
    psum x3 -> x0, blocking collectives: 22.8 us -> none  [the longest x1 9.55 us: shards(): squares = lax.psum(jnp.sum(hidden_wide * hidden_wide, axis=1), 'tp')]
    reduce_scatter x2 -> x0, waiting for transfers between devices: 22.7 us -> none  [combine(): return lax.psum_scatter(summed, 'tp', scatter_dimension=1, tiled=True)]
    all_gather x2 -> x0, blocking collectives: 21.1 us -> none  [dispatch(): whole_rows = lax.all_gather(token_rows, 'tp', axis=1, tiled=True)]
    reduce_sum x6 -> x0, other arithmetic: 18.1 us -> none  [the longest x2 15.1 us: combine(): summed = jnp.sum(picked.reshape(tok_count, top_count, width), axis=1)]
  transfers between devices with their start and end apart: 3 -> 0, of which waited for: 3 -> 0; matrix products, arithmetic and copies ran while one was open for 3% -> 0% of each run, Pallas kernels for 0% -> 0%
where the time goes in v1:
time: 297 us
  Pallas kernels  261 us (88%)
  matrix products  28.4 us (10%)
  local copies, waits for them, and re-layouts  4.75 us (2%)
    pallas_call x3, Pallas kernels, call(): pl.pallas_call(functools.partial(kernel, nz, nj, chunks), out_shape=outs,...  261 us
    dot_general x9, matrix products, dot(): lax.dot_general(a, b, (((ca,), (cb,)), ((), ())), preferred_element_type=...  28.4 us

profile of v1, /device:TPU:1, one launch (start us, length us, event | category | flops | bytes accessed | tf_op | source)
XLA Modules:
  0.0 296.9 jit_solution(17908878572004222718)
XLA Ops:
  0.6 0.0 copy-start
  0.6 0.8 convert_bitcast_fusion
  1.5 1.3 pad_maximum_fusion.own_ref
  2.7 1.3 concatenate.7.head_ref
  4.0 70.1 %dispatch_tokens.1 = (bf16[8,96,2048]{2,1,0:T(8,128)(2,1)}, f32[8,16,128]{2,1,0:T(8,128)}, f32[128,128]{1,0:T(8,128)}) custom-call(bf16[128,512]{1,0:T(8,128)(2,1)} %hidden_ref.5, f32[1,512]{1,0:T(1,128)} %bitcast.32, f32[16,128]{1,0:T(8,128)} %pad_maximum_fusion.own_ref), custom_call_target="tpu_custom_call" | custom-call | tf_op jit(solution)/shard_map/dispatch_tokens/pallas_call | solution.py:576
  74.1 0.0 copy-start.2
  74.1 0.0 copy-start.4
  74.1 4.3 %fusion = f32[768,384]{1,0:T(8,128)S(1)} fusion(bf16[768,2048]{1,0:T(8,128)(2,1)} %bitcast.37, bf16[384,2048]{1,0:T(8,128)(2,1)} %param.17), kind=kOutput, calls=%fused_computation.12 | convolution fusion | flops 1207959552 | bytes 5898240 | tf_op jit(solution)/shard_map/dot_general | solution.py:601
  78.5 0.0 copy-done.2
  78.5 0.0 copy-done.4
  78.5 0.0 copy-start.9
  78.5 2.9 multiply_convert_fusion.2
  81.3 0.0 copy-done.9
  81.3 0.0 copy-done
  81.4 3.5 %convolution_convert_fusion = bf16[768,2048]{1,0:T(8,128)(2,1)} fusion(bf16[768,384]{1,0:T(8,128)(2,1)S(1)} %get-tuple-element.22, bf16[384,2048]{1,0:T(8,128)(2,1)S(1)} %copy-done), kind=kOutput, calls=%fused_computation.1 | convolution fusion | flops 1209532416 | bytes 5308416 | tf_op jit(solution)/shard_map/dot_general | solution.py:601
  84.8 0.0 copy-done.7
  84.8 123.8 %combine_head_dispatch.1 = (bf16[128,512]{1,0:T(8,128)(2,1)}, f32[8,128]{1,0:T(8,128)}, f32[128,512]{1,0:T(8,128)}, bf16[8,96,2048]{2,1,0:T(8,128)(2,1)}) custom-call(bf16[8,96,2048]{2,1,0:T(8,128)(2,1)} %bitcast.31, f32[8,16,128]{2,1,0:T(8,128)} %get-tuple-element.14.meta_ref, bf16[128,512]{1,0:T(8,128)(2,1)} %hidden_ref.5, bf16[128,512]{1,0:T(8,128)(2,1)} %later_ref.1, ...), custom_call_target="tpu_custom_call" | custom-call | tf_op jit(solution)/shard_map/combine_head_dispatch/pallas_call | solution.py:576
  208.6 0.0 copy-start.6
  208.6 0.0 copy-start.8
  208.6 4.8 %multiply_convert_fusion = (bf16[768,384]{1,0:T(8,128)(2,1)S(1)}, bf16[768,384]{1,0:T(8,128)(2,1)S(1)}) fusion(f32[768,384]{1,0:T(8,128)} %copy-done.9, f32[768,384]{1,0:T(8,128)} %get-tuple-element.23, bf16[768,2048]{1,0:T(8,128)(2,1)} %bitcast.41, bf16[384,2048]{1,0:T(8,128)(2,1)S(1)} %copy-done), kind=kOutput, calls=%fused_computation.5 | convolution fusion | flops 1211793408 | bytes 8257536 | tf_op jit(solution)/shard_map/dot_general | solution.py:601
  213.5 1.2 slice_bitcast_fusion
  214.6 0.0 copy-done.6
  214.6 0.0 copy-done.8
  214.7 2.6 convolution_convert_fusion.1
  217.2 2.6 convolution_convert_fusion.2
  219.8 2.6 convolution_convert_fusion.3
  222.4 0.0 copy-done.1
  222.4 1.8 fusion.1
  224.2 3.4 %add_convert_fusion = bf16[768,2048]{1,0:T(8,128)(2,1)} fusion(f32[768,2048]{1,0:T(8,128)S(1)} %fusion.1, bf16[768,384]{1,0:T(8,128)(2,1)S(1)} %get-tuple-element.20, bf16[384,2048]{1,0:T(8,128)(2,1)S(1)} %copy-done.2), kind=kOutput, calls=%fused_computation | convolution fusion | flops 1211105280 | bytes 11599872 | tf_op jit(solution)/shard_map/dot_general | solution.py:601
  227.7 67.0 %combine_grad.1 = bf16[128,512]{1,0:T(8,128)(2,1)} custom-call(bf16[8,96,2048]{2,1,0:T(8,128)(2,1)} %bitcast.30, f32[8,16,128]{2,1,0:T(8,128)} %get-tuple-element.14.meta_ref, bf16[128,512]{1,0:T(8,128)(2,1)} %hidden_ref.5, f32[1,512]{1,0:T(1,128)} %bitcast.33, f32[128,128]{1,0:T(8,128)} %get-tuple-element.18.inv_ref, f32[128,512]{1,0:T(8,128)} %get-tuple-element.19.dout_ref), custom_call_target="tpu_custom_call" | custom-call | tf_op jit(solution)/shard_map/combine_grad/pallas_call | solution.py:576
  294.6 0.7 copy.18
  295.3 1.6 copy.19
  (6 shorter events, 0.0 us)
Async XLA Ops:
  0.6 80.7 %copy-start = (bf16[384,2048]{1,0:T(8,128)(2,1)S(1)}, bf16[384,2048]{1,0:T(8,128)(2,1)}, u32[]{:S(2)}) copy-start(bf16[384,2048]{1,0:T(8,128)(2,1)} %param.19) | copy-start | bytes 4718596
  74.1 4.3 %copy-start.2 = (bf16[384,2048]{1,0:T(8,128)(2,1)S(1)}, bf16[384,2048]{1,0:T(8,128)(2,1)}, u32[]{:S(2)}) copy-start(bf16[384,2048]{1,0:T(8,128)(2,1)} %param.18) | copy-start | bytes 4718596
  74.1 4.3 %copy-start.4 = (bf16[8,96,2048]{2,1,0:T(8,128)(2,1)S(1)}, bf16[8,96,2048]{2,1,0:T(8,128)(2,1)}, u32[]{:S(2)}) copy-start(bf16[8,96,2048]{2,1,0:T(8,128)(2,1)} %get-tuple-element.13) | copy-start | bytes 9437188
  78.5 2.9 copy-start.9
  81.3 3.5 %copy-start.7 = (bf16[768,384]{1,0:T(8,128)(2,1)}, bf16[768,384]{1,0:T(8,128)(2,1)S(1)}, u32[]{:S(2)}) copy-start(bf16[768,384]{1,0:T(8,128)(2,1)S(1)} %get-tuple-element.22) | copy-start | bytes 1769476
  208.6 6.0 %copy-start.6 = (bf16[8,96,2048]{2,1,0:T(8,128)(2,1)S(1)}, bf16[8,96,2048]{2,1,0:T(8,128)(2,1)}, u32[]{:S(2)}) copy-start(bf16[8,96,2048]{2,1,0:T(8,128)(2,1)} %get-tuple-element.17) | copy-start | bytes 9437188
  208.6 6.0 %copy-start.8 = (bf16[768,384]{1,0:T(8,128)(2,1)S(1)}, bf16[768,384]{1,0:T(8,128)(2,1)}, u32[]{:S(2)}) copy-start(bf16[768,384]{1,0:T(8,128)(2,1)} %copy-done.7) | copy-start | bytes 1769476
  214.6 2.6 copy-start.5
  219.8 2.6 copy-start.1
  227.6 67.0 %copy-start.3 = (bf16[128,512]{1,0:T(8,128)(2,1)S(1)}, bf16[128,512]{1,0:T(8,128)(2,1)}, u32[]{:S(2)}) copy-start(bf16[128,512]{1,0:T(8,128)(2,1)} %get-tuple-element.31) | copy-start | bytes 393220

commit v2 on v1

v2 whole, which is shorter than its diff:
```python
import functools

import jax
import jax.numpy as jnp
from jax import lax
from jax.experimental import pallas as pl
from jax.experimental.pallas import tpu as pltpu
from jax.sharding import PartitionSpec as P

FF = 768
EPS = 1e-06
LOSS_SCALE = 64.0
CAP = 12
LABELS = 4
QUAD = 4
LANES = 128
MESH = pl.DeviceIdType.MESH
F32 = jnp.float32
BF16 = jnp.bfloat16


def place(nj):
    ep = lax.axis_index("ep")
    t = lax.axis_index("tp")
    z = lax.div(ep, nj)
    j = lax.rem(ep, nj)
    return z, j, t


def z_order(nz):
    half = nz // 2
    order = []
    for back in range(half + 1):
        for k in (half - back, half + back):
            if 0 < k < nz and k not in order:
                order.append(k)
    return order


def rcopy(src, dst, send, recv, device):
    return pltpu.make_async_remote_copy(
        src_ref=src, dst_ref=dst, send_sem=send, recv_sem=recv, device_id=device, device_id_type=MESH
    )


def later(*args):
    return lambda: rcopy(*args)


def local_copy(*args):
    return lambda: pltpu.make_async_copy(*args)


def enter(nz, nj):
    z, j, t = place(nj)
    barrier = pltpu.get_barrier_semaphore()
    for k in range(1, nz):
        pl.semaphore_signal(
            barrier, inc=1, device_id={"ep": lax.rem(z + k, nz) * nj + j}, device_id_type=MESH
        )
    for k in range(1, nj):
        pl.semaphore_signal(
            barrier, inc=1, device_id={"ep": z * nj + lax.rem(j + k, nj)}, device_id_type=MESH
        )
    for k in range(1, 4):
        pl.semaphore_signal(barrier, inc=1, device_id={"tp": lax.rem(t + k, 4)}, device_id_type=MESH)
    pl.semaphore_wait(barrier, nz - 1 + nj - 1 + 3)


def column(t, f, chunks):
    return pl.ds(pl.multiple_of((t * chunks + f) * LANES, LANES), LANES)


def expert_keys(meta, z, ne):
    toks = meta.shape[1]
    names = (lax.broadcasted_iota(jnp.int32, (ne, toks), 0) + z * ne).astype(F32)
    named = jnp.zeros((ne, toks), F32)
    weight = jnp.zeros((ne, toks), F32)
    for k in range(8):
        hit = meta[k : k + 1, :] == names
        named = jnp.where(hit, 1.0, named)
        weight = jnp.where(hit, meta[8 + k : 9 + k, :], weight)
    earlier = (
        lax.broadcasted_iota(jnp.int32, (toks, toks), 0) < lax.broadcasted_iota(jnp.int32, (toks, toks), 1)
    ).astype(F32)
    rank = jnp.dot(named.astype(BF16), earlier.astype(BF16), preferred_element_type=F32)
    return jnp.where(named > 0.0, rank, -64.0), weight


def split(value, parts):
    out = []
    for _ in range(parts):
        out.append(value.astype(BF16))
        value = value - out[-1].astype(F32)
    return out


def build_pick(meta_ref, z, nz, ne, pick, weights):
    rows = QUAD * CAP
    row = lax.broadcasted_iota(jnp.int32, (ne, rows, LANES), 1).astype(F32)
    lane = lax.broadcasted_iota(jnp.int32, (ne * rows, LANES), 1)
    for q in range(nz // QUAD):

        def one(zq, held):
            key, weight = expert_keys(meta_ref[q * QUAD + zq], z, ne)
            key = key + (CAP * zq).astype(F32)
            at = row == key[:, None, :]
            hot = jnp.where(at, 1.0, 0.0).astype(BF16).reshape(ne * rows, LANES)
            pick[q, :, pl.ds(pl.multiple_of(zq * LANES, LANES), LANES)] = hot
            share = jnp.where(at, weight[:, None, :], 0.0).reshape(ne * rows, LANES)
            return held + jnp.sum(share, axis=1, keepdims=True)

        held = lax.fori_loop(0, QUAD, one, jnp.zeros((ne * rows, 1), F32))
        held = jnp.broadcast_to(held, (ne * rows, LANES))
        high, middle, low = [part.astype(F32) for part in split(held, 3)]
        value = jnp.where(lane == 12, high, jnp.where(lane == 13, middle, jnp.where(lane == 14, low, 0.0)))
        weights[q] = value.astype(BF16)


def build_place(meta_ref, z, nz, ne, place_hi, place_lo, place_one):
    wide = ne * QUAD * CAP
    expert = lax.broadcasted_iota(jnp.int32, (ne, wide), 0).astype(F32)
    lane = lax.broadcasted_iota(jnp.int32, (ne, wide), 1).astype(F32)
    start = expert * float(QUAD * CAP)
    spread = jnp.where((lane >= start) & (lane < start + float(QUAD * CAP)), 1.0, 0.0)
    base = jnp.sum(spread * start, axis=0, keepdims=True)
    within = lane[0:1] - base
    spread = spread.astype(BF16)
    fill = jnp.zeros((LANES - 3 * ne, LANES), F32)

    for q in range(nz // QUAD):

        def one(zq, carry):
            key, weight = expert_keys(meta_ref[q * QUAD + zq], z, ne)
            key = key + (CAP * zq).astype(F32)
            high, low = split(weight, 2)
            stack = jnp.concatenate([key, high.astype(F32), low.astype(F32), fill], axis=0)
            turned = jnp.transpose(stack).astype(BF16)
            at = jnp.dot(turned[:, 0:ne], spread, preferred_element_type=F32) == within
            where = pl.ds(pl.multiple_of(zq * LANES, LANES), LANES)
            highs = jnp.dot(turned[:, ne : 2 * ne], spread, preferred_element_type=F32)
            lows = jnp.dot(turned[:, 2 * ne : 3 * ne], spread, preferred_element_type=F32)
            place_hi[q, where, :] = jnp.where(at, highs, 0.0).astype(BF16)
            place_lo[q, where, :] = jnp.where(at, lows, 0.0).astype(BF16)
            place_one[q, where, :] = jnp.where(at, 1.0, 0.0).astype(BF16)
            return carry

        lax.fori_loop(0, QUAD, one, 0)


class Exchange:
    def __init__(self, buf, send, recv):
        self.t = lax.axis_index("tp")
        self.buf, self.send, self.recv = buf, send, recv

    def copies(self):
        t = self.t
        for k in range(1, 4):
            to = lax.rem(t + k, 4)
            yield later(
                self.buf.at[t], self.buf.at[t], self.send.at[k], self.recv.at[t], {"tp": to}
            ), later(self.buf.at[t], self.buf.at[to], self.send.at[k], self.recv.at[to], {"tp": to})

    def start(self, value):
        self.buf[self.t] = value
        for out, _ in self.copies():
            out().start()

    def total(self):
        for _, arriving in self.copies():
            arriving().wait_recv()
        return (self.buf[0] + self.buf[1]) + (self.buf[2] + self.buf[3])

    def total_again(self):
        return (self.buf[0] + self.buf[1]) + (self.buf[2] + self.buf[3])

    def drain(self):
        for out, _ in self.copies():
            out().wait_send()


def to_row(col):
    return jnp.transpose(jnp.broadcast_to(col, (LANES, LANES)))[0:8, :]


def to_columns(row):
    return jnp.transpose(jnp.broadcast_to(row, (LANES, LANES)))


DMA = pltpu.SemaphoreType.DMA


def lanes(f):
    return slice(f * LANES, (f + 1) * LANES)


class Refs:
    def __init__(self, names, refs):
        for name, ref in zip(names, refs):
            setattr(self, name, ref)


class Along:
    def __init__(self, count, axis, nj, send, recv):
        self.z, self.j, _ = place(nj)
        self.count, self.axis, self.nj, self.send, self.recv = count, axis, nj, send, recv

    def each(self):
        for k in z_order(self.count):
            if self.axis == "z":
                to = lax.rem(self.z + k, self.count)
                yield k, to, {"ep": to * self.nj + self.j}
            else:
                to = lax.rem(self.j + k, self.count)
                yield k, to, {"ep": self.z * self.nj + to}

    def copies(self, f, source, landing):
        me = self.z if self.axis == "z" else self.j
        for k, to, device in self.each():
            yield (
                later(source(to), landing(me), self.send.at[f, k], self.recv.at[f, me], device),
                later(source(to), landing(to), self.send.at[f, k], self.recv.at[f, to], device),
            )


class Dispatch:
    names = ["zbuf", "xsend", "xrecv", "zss", "zrs", "xss", "xrs", "xl"]

    @staticmethod
    def scratch(nz, nj, chunks):
        rows = nz * CAP
        return [
            pltpu.VMEM((chunks, nz, LANES, LANES), BF16),
            pltpu.VMEM((chunks, nj, 2, rows, LANES), BF16),
            pltpu.VMEM((chunks, 2, nj, rows, LANES), BF16),
            DMA((chunks, nz)),
            DMA((chunks, nz)),
            DMA((chunks, nj)),
            DMA((chunks, nj)),
            DMA((chunks,)),
        ]

    def __init__(self, nz, nj, chunks, pick, added, half, refs):
        self.nz, self.nj, self.chunks, self.pick_ref, self.added, self.half = nz, nj, chunks, pick, added, half
        self.z, self.j, self.t = place(nj)
        r = self.r = Refs(self.names, refs)
        self.along_z = Along(nz, "z", nj, r.zss, r.zrs)
        self.along_x = Along(nj, "x", nj, r.xss, r.xrs)

    def z_copies(self, f):
        return self.along_z.copies(f, lambda to: self.r.zbuf.at[f, self.z], lambda z: self.r.zbuf.at[f, z])

    def z_send(self, f, value):
        self.r.zbuf[f, self.z] = value
        for out, _ in self.z_copies(f):
            out().start()

    def pick(self, f):
        for _, arriving in self.z_copies(f):
            arriving().wait_recv()
        nj, rows = self.nj, QUAD * CAP
        for q in range(self.nz // QUAD):
            block = self.r.zbuf[f, q * QUAD : (q + 1) * QUAD].reshape(QUAD * LANES, LANES)
            got = jnp.dot(self.pick_ref[q], block, preferred_element_type=F32).astype(BF16)
            if self.added is not None:
                got = got + self.added[q]
            self.r.xsend[f, :, :, q * rows : (q + 1) * rows, :] = got.reshape(nj, 2, rows, LANES)
        for out, _ in self.x_copies(f):
            out().start()
        self.x_local(f)().start()

    def x_copies(self, f):
        r, half = self.r, self.half
        if half is None:
            return self.along_x.copies(f, lambda to: r.xsend.at[f, to], lambda j: r.xrecv.at[f, :, j])
        return self.along_x.copies(f, lambda to: r.xsend.at[f, to, half], lambda j: r.xrecv.at[f, half, j])

    def x_local(self, f):
        r, j, half = self.r, self.j, self.half
        if half is None:
            return local_copy(r.xsend.at[f, j], r.xrecv.at[f, :, j], r.xl.at[f])
        return local_copy(r.xsend.at[f, j, half], r.xrecv.at[f, half, j], r.xl.at[f])

    def x_wait(self, f):
        for _, arriving in self.x_copies(f):
            arriving().wait_recv()
        self.x_local(f)().wait()

    def drain(self):
        for f in range(self.chunks):
            for out, _ in self.z_copies(f):
                out().wait_send()
            for out, _ in self.x_copies(f):
                out().wait_send()


class Gather:
    names = ["yss", "yrs", "yl"]

    @staticmethod
    def scratch(chunks):
        return [DMA((chunks, 3)), DMA((chunks, 3)), DMA((chunks,))]

    def __init__(self, chunks, source, out, refs):
        self.chunks, self.source, self.out = chunks, source, out
        self.t = lax.axis_index("tp")
        self.r = Refs(self.names, refs)

    def copies(self, f):
        t, r, out = self.t, self.r, self.out
        half = lax.div(t, 2)
        mate = t + 1 - 2 * lax.rem(t, 2)
        across = 3 - t
        mine, theirs = out.at[:, :, column(t, f, self.chunks)], out.at[:, :, column(across, f, self.chunks)]
        far = out.at[:, :, column(3 - mate, f, self.chunks)]
        near = out.at[:, :, column(mate, f, self.chunks)]
        src, other = self.source.at[f, half], self.source.at[f, 1 - half]
        sends = (
            later(src, mine, r.yss.at[f, 0], r.yrs.at[f, 0], {"tp": mate}),
            later(other, mine, r.yss.at[f, 1], r.yrs.at[f, 1], {"tp": across}),
            later(theirs, theirs, r.yss.at[f, 2], r.yrs.at[f, 2], {"tp": mate}),
        )
        arrivals = (
            later(src, near, r.yss.at[f, 0], r.yrs.at[f, 0], {"tp": mate}),
            later(src, theirs, r.yss.at[f, 1], r.yrs.at[f, 1], {"tp": across}),
            later(src, far, r.yss.at[f, 2], r.yrs.at[f, 2], {"tp": mate}),
        )
        return sends, arrivals, local_copy(src, mine, r.yl.at[f])

    def send(self, f):
        sends, _, local = self.copies(f)
        sends[1]().start()
        sends[0]().start()
        local().start()

    def forward(self, f):
        sends, arrivals, _ = self.copies(f)
        arrivals[1]().wait_recv()
        sends[2]().start()

    def wait(self, f):
        _, arrivals, local = self.copies(f)
        arrivals[0]().wait_recv()
        arrivals[2]().wait_recv()
        local().wait()

    def chunk(self, f):
        rows = self.out.shape[0] * self.out.shape[1]
        parts = [self.out[:, :, wide(s, f, self.chunks)].reshape(rows, LANES) for s in range(4)]
        return jnp.concatenate(parts, axis=1)

    def relayed(self, f):
        self.copies(f)[0][2]().wait_send()

    def drain(self):
        for f in range(self.chunks):
            for out in self.copies(f)[0][:2]:
                out().wait_send()


def wide(s, f, chunks):
    return slice((s * chunks + f) * LANES, (s * chunks + f + 1) * LANES)


def weight_chunk(ref, f, chunks):
    return jnp.concatenate([ref[:, wide(s, f, chunks)] for s in range(4)], axis=1)


class Combine:
    names = ["yr", "ysum", "xs", "xr", "zs", "zr", "yss", "yrs", "xss", "xrs", "xl", "zss", "zrs"]

    @staticmethod
    def scratch(nz, nj, chunks):
        rows = nz * CAP
        return [
            pltpu.VMEM((chunks, 2, nj, rows, LANES), BF16),
            pltpu.VMEM((chunks, nj, rows, LANES), BF16),
            pltpu.VMEM((chunks, 2, nj, rows, LANES), BF16),
            pltpu.VMEM((chunks, nj, 2, rows, LANES), BF16),
            pltpu.VMEM((chunks, nz, LANES, LANES), BF16),
            pltpu.VMEM((chunks, nz, LANES, LANES), BF16),
            DMA((chunks, 3)),
            DMA((chunks, 3)),
            DMA((chunks, nj)),
            DMA((chunks, nj)),
            DMA((chunks,)),
            DMA((chunks, nz)),
            DMA((chunks, nz)),
        ]

    def __init__(self, nz, nj, chunks, value, places, refs):
        self.nz, self.nj, self.chunks, self.value, self.places = nz, nj, chunks, value, places
        self.z, self.j, self.t = place(nj)
        r = self.r = Refs(self.names, refs)
        self.along_z = Along(nz, "z", nj, r.zss, r.zrs)
        self.along_x = Along(nj, "x", nj, r.xss, r.xrs)

    def y_copies(self, f):
        t, r, n = self.t, self.r, self.chunks
        half = lax.div(t, 2)
        mate = t + 1 - 2 * lax.rem(t, 2)
        across = 3 - t
        sends = (
            later(self.value.at[:, :, column(mate, f, n)], r.yr.at[f, 0], r.yss.at[f, 0], r.yrs.at[f, 0],
                  {"tp": mate}),
            later(self.value.at[:, :, column(3 - mate, f, n)], r.yr.at[f, 1], r.yss.at[f, 1], r.yrs.at[f, 1],
                  {"tp": mate}),
            later(r.ysum.at[f], r.xs.at[f, half], r.yss.at[f, 2], r.yrs.at[f, 2], {"tp": across}),
        )
        last = later(r.ysum.at[f], r.xs.at[f, 1 - half], r.yss.at[f, 2], r.yrs.at[f, 2], {"tp": across})
        return sends, (sends[0], sends[1], last)

    def put(self, f, value):
        for s in range(4):
            part = value[:, lanes(s)].reshape(self.value.shape[0], self.value.shape[1], LANES)
            self.value[:, :, wide(s, f, self.chunks)] = part
        sends, _ = self.y_copies(f)
        sends[1]().start()
        sends[0]().start()

    def sent(self):
        for f in range(self.chunks):
            sends, _ = self.y_copies(f)
            sends[1]().wait_send()
            sends[0]().wait_send()

    def y_sum(self, f):
        t, r, n = self.t, self.r, self.chunks
        sends, arrivals = self.y_copies(f)
        arrivals[1]().wait_recv()

        def far(i, carry):
            own = self.value[i, :, column(3 - t, f, n)].astype(F32)
            r.ysum[f, i] = (own + r.yr[f, 1, i].astype(F32)).astype(BF16)
            return carry

        lax.fori_loop(0, self.nj, far, 0)
        sends[2]().start()
        arrivals[0]().wait_recv()
        half = lax.div(t, 2)

        def near(i, carry):
            own = self.value[i, :, column(t, f, n)].astype(F32)
            r.xs[f, half, i] = (own + r.yr[f, 0, i].astype(F32)).astype(BF16)
            return carry

        lax.fori_loop(0, self.nj, near, 0)

    def x_copies(self, f):
        return self.along_x.copies(f, lambda to: self.r.xs.at[f, :, to], lambda j: self.r.xr.at[f, j])

    def x_local(self, f):
        return local_copy(self.r.xs.at[f, :, self.j], self.r.xr.at[f, self.j], self.r.xl.at[f])

    def x_send(self, f):
        self.y_copies(f)[1][2]().wait_recv()
        for out, _ in self.x_copies(f):
            out().start()
        self.x_local(f)().start()

    def z_copies(self, f):
        return self.along_z.copies(f, lambda to: self.r.zs.at[f, to], lambda z: self.r.zr.at[f, z])

    def mix(self, f):
        for _, arriving in self.x_copies(f):
            arriving().wait_recv()
        self.x_local(f)().wait()
        rows = QUAD * CAP
        for q in range(self.nz // QUAD):
            got = self.r.xr[f, :, :, q * rows : (q + 1) * rows, :].reshape(self.nj * 2 * rows, LANES)
            part = jnp.dot(self.places[0][q], got, preferred_element_type=F32)
            for more in self.places[1:]:
                part = part + jnp.dot(more[q], got, preferred_element_type=F32)
            self.r.zs[f, q * QUAD : (q + 1) * QUAD] = part.astype(BF16).reshape(QUAD, LANES, LANES)
        for out, _ in self.z_copies(f):
            out().start()

    def result(self, f):
        for _, arriving in self.z_copies(f):
            arriving().wait_recv()
        total = self.r.zs[f, self.z].astype(F32)
        for k in range(1, self.nz):
            total = total + self.r.zr[f, lax.rem(self.z + k, self.nz)].astype(F32)
        return total

    def drain(self):
        for f in range(self.chunks):
            self.y_copies(f)[0][2]().wait_send()
            for out, _ in self.x_copies(f):
                out().wait_send()
            for out, _ in self.z_copies(f):
                out().wait_send()


def dot(a, b, ca, cb):
    return lax.dot_general(a, b, (((ca,), (cb,)), ((), ())), preferred_element_type=F32)


def parts(nz, nj, chunks, units):
    ne, nq = 2 * nj, nz // QUAD
    high, tall = ne * QUAD * CAP, QUAD * LANES
    rows = nj * nz * CAP
    out = {}
    out["meta"] = [pltpu.VMEM((nz, 16, LANES), F32), DMA((1, nz)), DMA((1, nz))]
    out["heads"] = [pltpu.VMEM((4, 8, chunks * LANES), BF16), DMA((4,)), DMA((4,))]
    for name in ("squares", "logits", "slopes"):
        out[name] = [pltpu.VMEM((4, 8, LANES), F32), DMA((4,)), DMA((4,))]
    out["picks"] = [pltpu.VMEM((nq, high, tall), BF16), pltpu.VMEM((nq, high, LANES), BF16)]
    out["places"] = [pltpu.VMEM((nq, tall, high), BF16)] * 3
    out["tokens"] = Dispatch.scratch(nz, nj, chunks)
    out["grads"] = Dispatch.scratch(nz, nj, chunks)
    out["small"] = Dispatch.scratch(nz, nj, 1)
    out["tokens_y"] = [pltpu.VMEM((nj, nz * CAP, 4 * chunks * LANES), BF16)] + Gather.scratch(chunks)
    out["grads_y"] = [pltpu.VMEM((nj, nz * CAP, 4 * chunks * LANES), BF16)] + Gather.scratch(chunks)
    out["value"] = [pltpu.VMEM((nj, nz * CAP, 4 * chunks * LANES), BF16)]
    out["forth"] = Combine.scratch(nz, nj, chunks)
    out["back"] = Combine.scratch(nz, nj, chunks)
    out["hidden"] = [pltpu.VMEM((rows, units), F32)] * 3 + [pltpu.VMEM((units, rows), BF16)]
    out["rows"] = [pltpu.VMEM((LANES, chunks * LANES), F32)] * 2
    return out


def block_kernel(nz, nj, chunks, hidden_ref, gain_ref, own_ref, later_ref, head_ref, labels_ref,
                 gate_ref, up_ref, down_ref, outcome_ref, loss_ref, grad_ref, ggate_ref, gup_ref, gdown_ref,
                 *scratch):
    groups, at = {}, 0
    for name, spec in parts(nz, nj, chunks, gate_ref.shape[0]).items():
        groups[name] = scratch[at : at + len(spec)]
        at += len(spec)
    z, j, t = place(nj)
    ne = 2 * nj
    width = 4 * chunks * LANES
    meta_ref, meta_ss, meta_rs = groups["meta"]
    heads_ref, heads_ss, heads_rs = groups["heads"]
    pick_ref, weights_ref = groups["picks"]
    (value_ref,) = groups["value"]
    gpre_ref, upre_ref, dact_ref, turned_ref = groups["hidden"]
    dout_ref, scaled_ref = groups["rows"]
    tokens = Dispatch(nz, nj, chunks, pick_ref, None, None, groups["tokens"])
    grads = Dispatch(nz, nj, chunks, pick_ref, None, None, groups["grads"])
    small = Dispatch(nz, nj, 1, pick_ref, weights_ref, lax.div(t, 2), groups["small"])
    tokens_y = Gather(chunks, tokens.r.xrecv, groups["tokens_y"][0], groups["tokens_y"][1:])
    grads_y = Gather(chunks, grads.r.xrecv, groups["grads_y"][0], groups["grads_y"][1:])
    forth = Combine(nz, nj, chunks, value_ref, groups["places"][:2], groups["forth"])
    back = Combine(nz, nj, chunks, value_ref, groups["places"][2:], groups["back"])

    enter(nz, nj)
    squares = Exchange(*groups["squares"])
    hidden = hidden_ref[...].astype(F32)
    squares.start(to_row(jnp.sum(hidden * hidden, axis=1, keepdims=True)))
    along = Along(nz, "z", nj, meta_ss, meta_rs)

    def meta_copies():
        return along.copies(0, lambda to: own_ref, lambda zz: meta_ref.at[zz])

    for out, _ in meta_copies():
        out().start()
    meta_ref[z] = own_ref[...]

    def head_copies():
        for k in range(1, 4):
            to = lax.rem(t + k, 4)
            yield (
                later(head_ref, heads_ref.at[t], heads_ss.at[k], heads_rs.at[t], {"tp": to}),
                later(head_ref, heads_ref.at[to], heads_ss.at[k], heads_rs.at[to], {"tp": to}),
            )

    inv = lax.rsqrt(to_columns(squares.total()[0:1, :]) / width + EPS)
    for f in range(chunks):
        normed = hidden_ref[:, lanes(f)].astype(F32) * inv * gain_ref[0:1, lanes(f)]
        tokens.z_send(f, normed.astype(BF16))
    for f in range(chunks):
        grads.z_send(f, later_ref[:, lanes(f)])
    for out, _ in head_copies():
        out().start()
    heads_ref[t] = head_ref[...]
    for _, arriving in meta_copies():
        arriving().wait_recv()
    build_pick(meta_ref, z, nz, ne, pick_ref, weights_ref)
    for step in range(chunks + 2):
        if step < chunks:
            tokens.pick(step)
        if 0 <= step - 1 < chunks:
            tokens.x_wait(step - 1)
            tokens_y.send(step - 1)
        if 0 <= step - 2 < chunks:
            tokens_y.forward(step - 2)
        if step == chunks - 1:
            build_place(meta_ref, z, nz, ne, *groups["places"])
    for f in range(chunks):
        tokens_y.wait(f)
        rows = tokens_y.chunk(f)
        gate = dot(rows, weight_chunk(gate_ref, f, chunks), 1, 1)
        up = dot(rows, weight_chunk(up_ref, f, chunks), 1, 1)
        if f:
            gate = gate + gpre_ref[...]
            up = up + upre_ref[...]
        gpre_ref[...] = gate
        upre_ref[...] = up
        if f < chunks - 1:
            grads.pick(f)
    gate, up = gpre_ref[...], upre_ref[...]
    active = gate * jax.nn.sigmoid(gate) * up
    active_low = active.astype(BF16)
    for f in range(chunks):
        forth.put(f, dot(active_low, weight_chunk(down_ref, f, chunks), 1, 0).astype(BF16))
    turned_ref[...] = jnp.transpose(active).astype(BF16)
    grads.pick(chunks - 1)
    for _, arriving in head_copies():
        arriving().wait_recv()
    early = chunks // 2
    for step in range(chunks + 2):
        if step < chunks:
            forth.y_sum(step)
        if step == chunks - 1:
            for f in range(early):
                grads.x_wait(f)
                grads_y.send(f)
        if 0 <= step - 1 < chunks:
            forth.x_send(step - 1)
        if 0 <= step - 2 < chunks:
            forth.mix(step - 2)
    for f in range(early):
        grads_y.forward(f)
    logits = jnp.zeros((8, LANES), F32)
    for f in range(chunks):
        outcome = (hidden_ref[:, lanes(f)].astype(F32) + forth.result(f)).astype(BF16)
        outcome_ref[:, lanes(f)] = outcome
        logits = logits + dot(head_ref[:, lanes(f)], outcome, 1, 1)
    sums = Exchange(*groups["logits"])
    sums.start(logits)
    for f in range(early, chunks):
        grads.x_wait(f)
        grads_y.send(f)
    logits = sums.total()
    row = lax.broadcasted_iota(jnp.int32, (8, LANES), 0)
    live = row < LABELS
    hot = jnp.where(row == labels_ref[0:1, :], 1.0, 0.0)
    powers = jnp.where(live, jnp.exp(jnp.where(live, logits, 0.0)), 0.0)
    totals = jnp.sum(powers, axis=0, keepdims=True)
    loss = jnp.log(totals) - jnp.sum(logits * hot, axis=0, keepdims=True)
    loss_ref[...] = jnp.broadcast_to(loss, (8, LANES))
    d_logits = (powers / totals - hot) * LOSS_SCALE
    pieces = [part.astype(F32)[0:LABELS] for part in split(d_logits, 3)]
    d_logits = jnp.concatenate(pieces + [jnp.zeros((LANES - 3 * LABELS, LANES), F32)], axis=0)
    d_logits = jnp.transpose(d_logits)
    small.z_send(0, d_logits.astype(BF16))
    head_rows = [heads_ref[s, 0:LABELS, :].astype(F32) for s in range(4)]
    blank = jnp.zeros((LANES - 3 * LABELS, chunks * LANES), F32)
    head_rows = [jnp.concatenate([rows, rows, rows, blank], axis=0).astype(BF16) for rows in head_rows]
    for f in range(chunks):
        term = jnp.zeros((LANES, LANES), F32)
        for label in range(LABELS):
            weight = head_ref[label : label + 1, lanes(f)].astype(F32)
            value = (d_logits[:, label : label + 1] + d_logits[:, LABELS + label : LABELS + label + 1]) + (
                d_logits[:, 2 * LABELS + label : 2 * LABELS + label + 1]
            )
            term = term + value * weight
        dout_ref[:, lanes(f)] = term + later_ref[:, lanes(f)].astype(F32)
    small.pick(0)
    for f in range(early, chunks):
        grads_y.forward(f)
    small.x_wait(0)
    tall = nj * nz * CAP
    slim = small.r.xrecv[0, lax.div(t, 2)].reshape(tall, LANES)
    weight = jnp.sum(slim[:, 3 * LABELS : 3 * LABELS + 3].astype(F32), axis=1, keepdims=True)
    for f in range(chunks):
        grads_y.wait(f)
        heads = jnp.concatenate([rows[:, lanes(f)] for rows in head_rows], axis=1)
        rounded = (dot(slim, heads, 1, 0) + grads_y.chunk(f).astype(F32)).astype(BF16)
        scaled = (weight * rounded.astype(F32)).astype(BF16)
        grads_y.relayed(f)
        for s in range(4):
            grads_y.out[:, :, wide(s, f, chunks)] = scaled[:, lanes(s)].reshape(nj, nz * CAP, LANES)
        part = dot(scaled, weight_chunk(down_ref, f, chunks), 1, 1)
        dact_ref[...] = part if f == 0 else dact_ref[...] + part
    gate, up, d_active = gpre_ref[...], upre_ref[...], dact_ref[...]
    sigma = jax.nn.sigmoid(gate)
    d_gate = d_active * up * sigma * (1.0 + gate * (1.0 - sigma))
    d_up = d_active * gate * sigma
    gpre_ref[...] = d_gate
    upre_ref[...] = d_up
    d_gate, d_up = d_gate.astype(BF16), d_up.astype(BF16)
    forth.sent()
    for f in range(chunks):
        total = dot(d_gate, weight_chunk(gate_ref, f, chunks), 1, 0)
        total = total + dot(d_up, weight_chunk(up_ref, f, chunks), 1, 0)
        back.put(f, total.astype(BF16))

    def weight_grad(left, right, out):
        def one(i, carry):
            where = pl.ds(pl.multiple_of(i * 2 * LANES, 2 * LANES), 2 * LANES)
            got = right[:, :, where].reshape(tall, 2 * LANES)
            out[:, where] = jnp.dot(left[...], got, preferred_element_type=F32).astype(BF16)
            return carry

        lax.fori_loop(0, width // (2 * LANES), one, 0)

    weight_grad(turned_ref, grads_y.out, gdown_ref)
    turned_ref[...] = jnp.transpose(gpre_ref[...]).astype(BF16)
    weight_grad(turned_ref, tokens_y.out, ggate_ref)
    turned_ref[...] = jnp.transpose(upre_ref[...]).astype(BF16)
    weight_grad(turned_ref, tokens_y.out, gup_ref)
    for step in range(chunks + 2):
        if step < chunks:
            back.y_sum(step)
        if 0 <= step - 1 < chunks:
            back.x_send(step - 1)
        if 0 <= step - 2 < chunks:
            back.mix(step - 2)
    slope = jnp.zeros((LANES, LANES), F32)
    for f in range(chunks):
        scaled = back.result(f) * gain_ref[0:1, lanes(f)]
        scaled_ref[:, lanes(f)] = scaled
        slope = slope + scaled * hidden_ref[:, lanes(f)].astype(F32)
    slopes = Exchange(*groups["slopes"])
    slopes.start(to_row(jnp.sum(slope, axis=1, keepdims=True)))
    slope = to_columns(slopes.total()[0:1, :]) / width
    inv = lax.rsqrt(to_columns(squares.total_again()[0:1, :]) / width + EPS)
    cube = inv * inv * inv
    for f in range(chunks):
        d_hidden = inv * scaled_ref[:, lanes(f)] - hidden_ref[:, lanes(f)].astype(F32) * cube * slope
        grad_ref[:, lanes(f)] = (dout_ref[:, lanes(f)] + d_hidden).astype(BF16)
    back.sent()
    for f in range(chunks):
        tokens_y.relayed(f)
    for copies in (meta_copies, head_copies):
        for out, _ in copies():
            out().wait_send()
    for part in (squares, sums, slopes, tokens, grads, small, tokens_y, grads_y, forth, back):
        part.drain()


def shards(nz, nj, hidden_in, norm_gain, expert_ids, routing_weight, labels, grad_later, head_weight,
           gate_weight, up_weight, down_weight):
    chunks = hidden_in.shape[1] // LANES
    vmem = pl.BlockSpec(memory_space=pltpu.VMEM)
    own = jnp.concatenate([expert_ids.T.astype(F32), routing_weight.T], axis=0)
    head = jnp.concatenate([head_weight.T, jnp.zeros_like(head_weight.T)], axis=0)
    args = (hidden_in, norm_gain[None, :], own, grad_later, head, labels[None, :],
            gate_weight, up_weight, down_weight)
    outs = [
        jax.ShapeDtypeStruct(hidden_in.shape, BF16),
        jax.ShapeDtypeStruct((8, LANES), F32),
        jax.ShapeDtypeStruct(hidden_in.shape, BF16),
    ] + [jax.ShapeDtypeStruct(gate_weight.shape, BF16)] * 3
    scratch = [spec for group in parts(nz, nj, chunks, gate_weight.shape[0]).values() for spec in group]
    outcome, loss, grad_input, grad_gate, grad_up, grad_down = pl.pallas_call(
        functools.partial(block_kernel, nz, nj, chunks),
        out_shape=outs,
        in_specs=[vmem] * len(args),
        out_specs=[vmem] * len(outs),
        scratch_shapes=scratch,
        name="expert_block",
        compiler_params=pltpu.CompilerParams(
            collective_id=1, has_side_effects=True, vmem_limit_bytes=67043328
        ),
    )(*args)
    return loss[0], outcome, grad_input, grad_gate, grad_up, grad_down


def solution(mesh, nj=8):
    nz = mesh.shape["ep"] // nj
    in_specs = (
        P("ep", "tp"),
        P("tp"),
        P("ep", None),
        P("ep", None),
        P("ep"),
        P("ep", "tp"),
        P("tp", None),
        P(("ep", "tp"), None),
        P(("ep", "tp"), None),
        P(("ep", "tp"), None),
    )
    out_specs = (
        P("ep"),
        P("ep", "tp"),
        P("ep", "tp"),
        P(("ep", "tp"), None),
        P(("ep", "tp"), None),
        P(("ep", "tp"), None),
    )
    return jax.shard_map(
        functools.partial(shards, nz, nj), mesh=mesh, in_specs=in_specs, out_specs=out_specs, check_vma=False
    )
```

time: 297 us -> 233 us (0.78)
  Pallas kernels: 261 us -> 218 us
  matrix products: 28.4 us -> 0 us
  local copies, waits for them, and re-layouts: 4.75 us -> 11.6 us
    pallas_call x3 -> x1, Pallas kernels: 261 us -> 218 us  [shards(): pl.pallas_call(functools.partial(block_kernel, nz, nj, chunks), out_shape...]
    dot_general x9 -> x0, matrix products: 28.4 us -> none  [dot(): lax.dot_general(a, b, (((ca,), (cb,)), ((), ())), preferred_element_type=...]
    unnamed x22 -> x9, local copies, waits for them, and re-layouts: 2.28 us -> 9.1 us
where the time goes in v2:
time: 233 us
  Pallas kernels  218 us (94%)
  local copies, waits for them, and re-layouts  11.6 us (5%)
    pallas_call x1, Pallas kernels, shards(): pl.pallas_call(functools.partial(block_kernel, nz, nj, chunks), out_shape...  218 us
    unnamed x9, local copies, waits for them, and re-layouts  9.1 us

profile of v2, /device:TPU:1, one launch (start us, length us, event | category | flops | bytes accessed | tf_op | source)
XLA Modules:
  0.0 232.6 jit_solution(3905700739268679051)
XLA Ops:
  0.6 0.7 convert_bitcast_fusion
  1.3 1.3 pad_maximum_fusion.own_ref
  2.6 1.3 concatenate.7.head_ref
  3.9 218.4 %expert_block.1 = (bf16[128,512]{1,0:T(8,128)(2,1)}, f32[8,128]{1,0:T(8,128)}, bf16[128,512]{1,0:T(8,128)(2,1)}, bf16[384,2048]{1,0:T(8,128)(2,1)}, bf16[384,204...) custom-call(bf16[128,512]{1,0:T(8,128)(2,1)} %hidden_ref.1, f32[1,512]{1,0:T(1,128)} %bitcast.10, ...), custom_call_target="tpu_custom_call" | custom-call | tf_op jit(solution)/shard_map/expert_block/pallas_call | solution.py:748
  222.3 1.2 slice_bitcast_fusion
  223.5 1.6 copy.21
  225.0 1.6 copy.22
  226.6 0.0 copy-start.1
  226.6 2.8 %copy.23 = bf16[384,2048]{1,0:T(8,128)(2,1)} copy(bf16[384,2048]{1,0:T(8,128)(2,1)} %get-tuple-element.27) | data formatting | bytes 3145728
  229.5 0.0 copy-done.1
  229.5 0.0 copy-start
  229.5 1.1 copy.24
  230.6 0.8 copy-done
  231.4 1.1 copy.25
Async XLA Ops:
  226.6 2.9 %copy-start.1 = (bf16[384,2048]{1,0:T(8,128)(2,1)S(1)}, bf16[384,2048]{1,0:T(8,128)(2,1)}, u32[]{:S(2)}) copy-start(bf16[384,2048]{1,0:T(8,128)(2,1)} %get-tuple-element.28) | copy-start | bytes 4718596
  229.5 2.0 copy-start
